TPU v7x, 512 devices: a whole 4x4x16 slice. The times are simulated.
512 devices in a mesh: gz: 16 (over z), xy: 32 (over x, y, core).
Axes of the slice: x: 4, y: 4, z: 16, core: 2. Of those that a mesh axis runs over, the one named last changes fastest.
Arguments:
- source: float32 [512, 128, 512], P('gz', 'xy'), may hold values from -6 to 6
- potential: float32 [512, 128, 512], P('gz', 'xy'), may hold values from -6 to 6
Outputs:
- new_potential: float32 [512, 128, 512], P('gz', 'xy')
All inputs are finite; a program needn't handle non-finite values.
Results may differ from a plain program's by a relative error of at most 0.0003.
Values sent between devices are 32-bit elements; how exact they have to be, the bound alone decides.
A program may use at most 64 MiB of HBM per device.

v0:
```python
import math

import jax
import jax.numpy as jnp
from jax import lax
from jax.sharding import PartitionSpec as P

SWEEPS = 2
SCREEN = 64


OMEGA = 0.8
HIGH = lax.Precision.HIGHEST


def with_halo(value, sides, width):
    for axis, dim in sides:
        size, length = (lax.axis_size(axis), value.shape[dim])
        up = [(i, (i + 1) % size) for i in range(size - 1)]
        down = [(j, i) for i, j in up]
        last = lax.slice_in_dim(value, length - width, length, axis=dim)
        initial = lax.slice_in_dim(value, 0, width, axis=dim)
        before = lax.ppermute(last, axis, up)
        after = lax.ppermute(initial, axis, down)
        value = jnp.concatenate([before, value, after], axis=dim)
    return value


def carried_in(value, axis, join, neutral, backward):
    count, mine = (lax.axis_size(axis), lax.axis_index(axis))
    pieces = jax.tree.map(lambda part: lax.all_gather(part, axis), value)
    if backward:
        pieces = jax.tree.map(lambda part: part[::-1], pieces)
        mine = count - 1 - mine
    total = jax.tree.map(
        lambda part, zero: jnp.full_like(part, 0) + jnp.asarray(zero, part.dtype), value, neutral
    )

    def step(position, total):
        longer = join(total, jax.tree.map(lambda part: part[position], pieces))
        return jax.tree.map(lambda new, old: jnp.where(position < mine, new, old), longer, total)

    return lax.fori_loop(0, count - 1, step, total)


def sine_table(count):
    idx = jnp.arange(1, count + 1, dtype=jnp.int32)
    turns = idx[:, None] * idx[None, :] % (2 * (count + 1))
    return math.sqrt(2.0 / (count + 1)) * jnp.sin(math.pi / (count + 1) * turns.astype(jnp.float32))


def eigenvalues(count, taken):
    idx = (jnp.arange(taken, dtype=jnp.int32) + 1).astype(jnp.float32)
    return 2.0 - 2.0 * jnp.cos(math.pi / (count + 1) * idx)


def relax(extended, rhs, kappa):
    centre = extended[1:-1, 1:-1]
    padded_y = jnp.pad(centre, ((0, 0), (0, 0), (1, 1)))
    total = extended[2:, 1:-1] + extended[:-2, 1:-1] + extended[1:-1, 2:] + extended[1:-1, :-2]
    total = total + padded_y[:, :, 2:] + padded_y[:, :, :-2]
    centre_weight = 6.0 + kappa
    return centre + OMEGA * (rhs - (centre_weight * centre - total)) / centre_weight


def smooth(field, source, kappa):
    for sweep in range(SWEEPS):
        extended = with_halo(field, (("gz", 0), ("xy", 1)), 1)
        field = relax(extended, source, kappa)
    return field


def compose(earlier, later):
    return (earlier[0] * later[0], later[0] * earlier[1] + later[1])


def solve_columns(rhs, diag):
    planes = rhs.shape[0]
    first = lax.axis_index("gz") * planes
    decay = jnp.log(0.5 * diag + jnp.sqrt(0.25 * diag * diag - 1.0))
    factor = jnp.exp(-decay)
    level = (first + jnp.arange(planes, dtype=jnp.int32)).astype(jnp.float32)
    level = level.reshape((planes,) + (1,) * diag.ndim)
    coeff = (
        factor * jnp.expm1(-2.0 * (level + 1.0) * decay) / jnp.expm1(-2.0 * (level + 2.0) * decay)
    )
    ones = jnp.ones_like(diag)
    zeros = jnp.zeros_like(diag)

    def up_step(carry, item):
        pivot, value = item
        return ((pivot * carry[0], pivot * (value + carry[1])), None)

    (lift, offset), unused = lax.scan(up_step, (ones, zeros), (coeff, rhs))
    prefix = carried_in((lift, offset), "gz", compose, (ones, zeros), False)

    def fill_up(carry, item):
        pivot, value = item
        carry = pivot * (value + carry)
        return (carry, carry)

    unused, eliminated = lax.scan(fill_up, prefix[1], (coeff, rhs))

    def down_step(carry, item):
        pivot, value = item
        return ((pivot * carry[0], value + pivot * carry[1]), None)

    (lift_top, offset_top), unused = lax.scan(
        down_step, (ones, zeros), (coeff, eliminated), reverse=True
    )
    suffix = carried_in((lift_top, offset_top), "gz", compose, (ones, zeros), True)

    def fill_down(carry, item):
        pivot, value = item
        carry = value + pivot * carry
        return (carry, carry)

    unused, solved = lax.scan(fill_down, suffix[1], (coeff, eliminated), reverse=True)
    return solved


def coarse_solve(coarse, kappa):
    planes, rows, cols = coarse.shape
    groups = lax.axis_size("xy")
    total_rows = rows * groups
    table_x = sine_table(total_rows)
    table_y = sine_table(cols)
    modes_x = eigenvalues(total_rows, total_rows)
    whole = lax.all_gather(coarse, "xy", axis=1, tiled=True)
    spec = jnp.dot(whole.reshape(-1, cols), table_y, precision=HIGH).reshape(
        planes, total_rows, cols
    )
    spec = jnp.einsum("ax,zxy->zay", table_x, spec, precision=HIGH)
    modes_y = eigenvalues(cols, cols)
    diag = 2.0 + modes_x[:, None] + modes_y[None, :] + 4.0 * kappa
    solved = solve_columns(4.0 * spec, diag)
    own_rows = lax.dynamic_slice_in_dim(table_x, lax.axis_index("xy") * rows, rows, 0)
    back = jnp.einsum("xa,zay->zxy", own_rows, solved, precision=HIGH)
    return jnp.dot(back.reshape(-1, cols), table_y, precision=HIGH).reshape(planes, rows, cols)


def body(source, potential):
    kappa = 1.0 / (SCREEN * SCREEN)
    centre_weight = 6.0 + kappa
    height, width, depth_y = source.shape
    field = smooth(potential, source, kappa)
    extended = with_halo(field, (("gz", 0), ("xy", 1)), 1)
    padded_y = jnp.pad(field, ((0, 0), (0, 0), (1, 1)))
    total = extended[2:, 1:-1] + extended[:-2, 1:-1] + extended[1:-1, 2:] + extended[1:-1, :-2]
    total = total + padded_y[:, :, 2:] + padded_y[:, :, :-2]
    residual = source - (centre_weight * field - total)
    coarse = residual.reshape(height // 2, 2, width // 2, 2, depth_y // 2, 2).mean(axis=(1, 3, 5))
    correction = coarse_solve(coarse, kappa)
    lifted = jnp.broadcast_to(
        correction[:, None, :, None, :, None], (height // 2, 2, width // 2, 2, depth_y // 2, 2)
    )
    field = field + lifted.reshape(height, width, depth_y)
    return smooth(field, source, kappa)


def solution(mesh):
    placed = (P("gz", "xy", None), P("gz", "xy", None))
    return jax.shard_map(
        body, mesh=mesh, in_specs=placed, out_specs=P("gz", "xy", None), check_vma=False
    )
```

profile of v0, /device:TPU:1, one launch (start us, length us, event | category | flops | bytes accessed | tf_op | source)
XLA Modules:
  0.0 554.1 jit_solution(7522685730354100004)
XLA Ops:
  7.3 1.3 collective-permute-start
  8.6 5.0 collective-permute-start.1
  13.6 1.0 copy.26
  14.7 8.6 %collective-permute-start.2 = (f32[34,1,512]{2,0,1:T(8,128)S(1)}, f32[34,1,512]{2,0,1:T(8,128)S(1)}, u32[]{:S(2)}, u32[]{:S(2)}) collective-permute-start(f32[34,1,512]{2,0,1:T(8,128)S(1)} %get-tuple-element.611), channel_id=1, source_target_pairs={{1,0},{2,1},{3,2},{4,3},{5,4},{6,5},{7,6},{8,7},{9,8},{10,9},{11,1... | collective-permute-start | bytes 208904 | tf_op jit(solution)/shard_map/ppermute | solution.py:24
  23.3 1.9 collective-permute-start.3
  25.2 1.5 collective-permute-done.3
  26.7 1.2 fusion.13
  28.0 1.3 collective-permute-start.4
  29.3 4.5 collective-permute-start.5
  34.6 2.7 collective-permute-start.6
  37.3 4.4 collective-permute-start.7
  41.9 1.3 collective-permute-done.7
  43.1 1.2 fusion.19
  44.4 1.3 collective-permute-start.8
  45.7 4.5 collective-permute-start.9
  51.0 1.9 collective-permute-start.10
  53.0 5.1 collective-permute-start.11
  58.3 1.3 collective-permute-done.11
  59.6 1.2 fusion.23
  60.8 18.1 %reshape.130 = f32[16,2,2,2,256,2]{5,4,1,0,3,2:T(8,128)} reshape(f32[32,4,512]{2,0,1:T(8,128)S(1)} %fusion.23) | data formatting | bytes 524288 | tf_op jit(solution)/shard_map/reshape | solution.py:152
  78.8 7.0 %reduce_sum.9 = f32[16,2,256]{2,0,1:T(8,128)S(1)} reduce(f32[16,2,2,2,256,2]{5,4,1,0,3,2:T(8,128)} %reshape.130, f32[]{:T(128)} %constant.201.clone.1), dimensions={1,3,5}, to_apply=%region_0.1 | reduce | flops 57344 | bytes 294916 | tf_op jit(solution)/shard_map/reduce_sum | solution.py:152
  87.6 67.6 %all-gather.10.cloned.1.call-done = f32[16,64,256]{2,0,1:T(8,128)} async-done(((f32[16,2,256]{2,0,1:T(8,128)}), f32[16,64,256]{2,0,1:T(8,128)}) %all-gather.10.cloned.1.call-update) | async-done | bytes 1048592 | tf_op jit(solution)/shard_map/all_gather | solution.py:129
  155.2 3.8 fusion.6
  158.9 1.3 fusion.5
  162.6 59.9 %all-gather.14.cloned.1.call-done = f32[1024,256]{1,0:T(8,128)} async-done(((f32[64,256]{1,0:T(8,128)}), f32[1024,256]{1,0:T(8,128)}) %all-gather.14.cloned.1.call-update) | async-done | bytes 1048592 | tf_op jit(solution)/shard_map/all_gather | solution.py:31
  222.5 70.0 %all-gather.12.cloned.1.call-done = f32[1024,256]{1,0:T(8,128)} async-done(((f32[64,256]{1,0:T(8,128)}), f32[1024,256]{1,0:T(8,128)}) %all-gather.12.cloned.1.call-update) | async-done | bytes 1048592 | tf_op jit(solution)/shard_map/all_gather | solution.py:31
  292.6 14.0 %while.89 = (s32[]{:T(128)}, f32[64,256]{1,0:T(8,128)S(1)}, s32[]{:T(128)}, f32[16,64,256]{2,1,0:T(8,128)}, f32[16,64,256]{2,1,0:T(8,128)}, /*index=5*/s32[]{:T(128)}, s32[]{:T(128)}) while((s32[]{:T(128)}, f32[64,256]{1,0:T(8,128)S(1)}, s32[]{:T(128)}, f32[16,64,256]{2,1,0:T(8,128)}, f32[16,64,256]{2,1,0:T(8,128)}, ...), condition=%wide.region_4.5_spmd.clone, body=%wide.region_3.4_spmd.clone.sunk | while | flops 65540 | bytes 262245 | solution.py:43
  295.4 0.9 fusion.116
  296.3 0.9 fusion.116
  304.7 0.9 fusion.116
  307.4 23.3 %while.90 = (s32[]{:T(128)}, f32[64,256]{1,0:T(8,128)S(1)}, f32[64,256]{1,0:T(8,128)}, f32[16,64,256]{2,1,0:T(8,128)S(1)}, f32[16,64,256]{2,1,0:T(8,128)S(1)}, /*index=5*/s32[]{:T(128)}, s32[]{:T(128)}, s32[]{:T(128)}) while((s32[]{:T(128)}, f32[64,256]{1,0:T(8,128)S(1)}, f32[64,256]{1,0:T(8,128)}, f32[16,64,256]{2,1,0:T(8,128)S(1)}, ...), condition=%wide.region_8.9_spmd.clone, body=%wide.region_7.8_spmd.clone.sunk | while | flops 81924 | bytes 393327 | solution.py:108
  308.1 1.5 bitcast_add_fusion.6
  309.6 1.5 bitcast_add_fusion.6
  311.1 1.5 bitcast_add_fusion.6
  312.6 1.5 bitcast_add_fusion.6
  314.1 1.5 bitcast_add_fusion.6
  315.6 1.5 bitcast_add_fusion.6
  317.1 1.5 bitcast_add_fusion.6
  318.6 1.5 bitcast_add_fusion.6
  320.1 1.5 bitcast_add_fusion.6
  321.6 1.5 bitcast_add_fusion.6
  323.1 1.5 bitcast_add_fusion.6
  324.6 1.5 bitcast_add_fusion.6
  326.1 1.5 bitcast_add_fusion.6
  327.7 1.5 bitcast_add_fusion.6
  329.2 1.5 bitcast_add_fusion.6
  332.1 67.3 %all-gather.16.cloned.1.call-done = f32[1024,256]{1,0:T(8,128)} async-done(((f32[64,256]{1,0:T(8,128)}), f32[1024,256]{1,0:T(8,128)}) %all-gather.16.cloned.1.call-update) | async-done | bytes 1048592 | tf_op jit(solution)/shard_map/all_gather | solution.py:31
  399.4 1.3 rev.6
  400.7 68.6 %all-gather.18.cloned.1.call-done = f32[1024,256]{1,0:T(8,128)} async-done(((f32[64,256]{1,0:T(8,128)}), f32[1024,256]{1,0:T(8,128)}) %all-gather.18.cloned.1.call-update) | async-done | bytes 1048592 | tf_op jit(solution)/shard_map/all_gather | solution.py:31
  469.3 2.4 rev.7
  471.6 13.6 %while.91 = (s32[]{:T(128)}, f32[64,256]{1,0:T(8,128)S(1)}, s32[]{:T(128)}, f32[16,64,256]{2,1,0:T(8,128)S(1)}, f32[16,64,256]{2,1,0:T(8,128)}, /*index=5*/s32[]{:T(128)}, s32[]{:T(128)}) while((s32[]{:T(128)}, f32[64,256]{1,0:T(8,128)S(1)}, s32[]{:T(128)}, f32[16,64,256]{2,1,0:T(8,128)S(1)}, f32[16,64,256]{2,1,0:T(8,128)}, ...), condition=%wide.region_10.11_spmd.clone, body=%wide.region_9.10_spmd.clone.sunk | while | flops 65540 | bytes 262245 | solution.py:43
  486.6 1.3 fusion.59
  488.0 6.4 %broadcast_in_dim.31 = f32[16,2,2,2,256,2]{5,4,1,0,3,2:T(8,128)} broadcast(f32[16,2,256]{2,0,1:T(8,128)S(1)} %fusion.59), dimensions={0,2,4} | broadcast | bytes 294912 | tf_op jit(solution)/shard_map/broadcast_in_dim | solution.py:154
  494.4 12.7 %reshape.131 = f32[32,4,512]{2,0,1:T(8,128)S(1)} reshape(f32[16,2,2,2,256,2]{5,4,1,0,3,2:T(8,128)} %broadcast_in_dim.31) | data formatting | bytes 524288 | tf_op jit(solution)/shard_map/reshape | solution.py:157
  507.2 1.3 collective-permute-start.12
  508.5 4.0 collective-permute-start.13
  513.3 13.2 %collective-permute-start.14 = (f32[34,1,512]{2,0,1:T(8,128)S(1)}, f32[34,1,512]{2,0,1:T(8,128)S(1)}, u32[]{:S(2)}, u32[]{:S(2)}) collective-permute-start(f32[34,1,512]{2,0,1:T(8,128)S(1)} %get-tuple-element.605), channel_id=1, source_target_pairs={{1,0},{2,1},{3,2},{4,3},{5,4},{6,5},{7,6},{8,7},{9,8},{10,9},{11,1... | collective-permute-start | bytes 208904 | tf_op jit(solution)/shard_map/ppermute | solution.py:24
  526.5 3.0 collective-permute-start.15
  529.7 1.3 collective-permute-done.15
  531.2 1.3 collective-permute-start.16
  532.5 4.5 collective-permute-start.17
  537.9 1.9 collective-permute-start.18
  539.8 5.1 collective-permute-start.19
  545.2 1.3 collective-permute-done.19
  (146 shorter events, 40.0 us)
Async XLA Ops:
  6.5 148.6 %all-gather.10.cloned.1.call-start = ((), (), s32[]{:S(2)}) async-start(), calls=%async_computation | async-start | bytes 1081344 | tf_op jit(solution)/shard_map/all_gather | solution.py:129
  7.3 7.4 %collective-permute-start = (f32[1,4,512]{2,0,1:T(1,128)S(1)}, f32[1,4,512]{2,0,1:T(1,128)S(1)}, u32[]{:S(2)}, u32[]{:S(2)}) collective-permute-start(f32[1,4,512]{2,0,1:T(1,128)S(1)} %copy.19), channel_id=1, source_target_pairs={{32,0},{64,32},{96,64},{128,96},{160,128},{192,160},{224,192},{256... | collective-permute-start | bytes 24584 | tf_op jit(solution)/shard_map/ppermute | solution.py:24
  8.6 6.1 %collective-permute-start.1 = (f32[1,4,512]{2,0,1:T(1,128)S(1)}, f32[1,4,512]{2,0,1:T(1,128)S(1)}, u32[]{:S(2)}, u32[]{:S(2)}) collective-permute-start(f32[1,4,512]{2,0,1:T(1,128)S(1)} %copy.21), channel_id=1, source_target_pairs={{0,32},{32,64},{64,96},{96,128},{128,160},{160,192},{192,224},{224... | collective-permute-start | bytes 24584 | tf_op jit(solution)/shard_map/ppermute | solution.py:23
  14.7 10.6 %collective-permute-start.2 = (f32[34,1,512]{2,0,1:T(8,128)S(1)}, f32[34,1,512]{2,0,1:T(8,128)S(1)}, u32[]{:S(2)}, u32[]{:S(2)}) collective-permute-start(f32[34,1,512]{2,0,1:T(8,128)S(1)} %get-tuple-element.611), channel_id=1, source_target_pairs={{1,0},{2,1},{3,2},{4,3},{5,4},{6,5},{7,6},{8,7},{9,8},{10,9},{11,1... | collective-permute-start | bytes 208904 | tf_op jit(solution)/shard_map/ppermute | solution.py:24
  23.3 3.4 collective-permute-start.3
  28.0 5.8 %collective-permute-start.4 = (f32[1,4,512]{2,0,1:T(1,128)S(1)}, f32[1,4,512]{2,0,1:T(1,128)S(1)}, u32[]{:S(2)}, u32[]{:S(2)}) collective-permute-start(f32[1,4,512]{2,0,1:T(1,128)S(1)} %get-tuple-element.620), channel_id=1, source_target_pairs={{32,0},{64,32},{96,64},{128,96},{160,128},{192,160},{224,192},{256... | collective-permute-start | bytes 24584 | tf_op jit(solution)/shard_map/ppermute | solution.py:24
  29.3 5.3 collective-permute-start.5
  34.6 7.3 %collective-permute-start.6 = (f32[34,1,512]{2,0,1:T(8,128)S(1)}, f32[34,1,512]{2,0,1:T(8,128)S(1)}, u32[]{:S(2)}, u32[]{:S(2)}) collective-permute-start(f32[34,1,512]{2,0,1:T(8,128)S(1)} %get-tuple-element.609), channel_id=1, source_target_pairs={{1,0},{2,1},{3,2},{4,3},{5,4},{6,5},{7,6},{8,7},{9,8},{10,9},{11,1... | collective-permute-start | bytes 208904 | tf_op jit(solution)/shard_map/ppermute | solution.py:24
  37.3 5.8 %collective-permute-start.7 = (f32[34,1,512]{2,0,1:T(8,128)S(1)}, f32[34,1,512]{2,0,1:T(8,128)S(1)}, u32[]{:S(2)}, u32[]{:S(2)}) collective-permute-start(f32[34,1,512]{2,0,1:T(8,128)S(1)} %get-tuple-element.610), channel_id=1, source_target_pairs={{0,1},{1,2},{2,3},{3,4},{4,5},{5,6},{6,7},{7,8},{8,9},{9,10},{10,1... | collective-permute-start | bytes 208904 | tf_op jit(solution)/shard_map/ppermute | solution.py:23
  44.4 5.8 %collective-permute-start.8 = (f32[1,4,512]{2,0,1:T(1,128)S(1)}, f32[1,4,512]{2,0,1:T(1,128)S(1)}, u32[]{:S(2)}, u32[]{:S(2)}) collective-permute-start(f32[1,4,512]{2,0,1:T(1,128)S(1)} %get-tuple-element.618), channel_id=1, source_target_pairs={{32,0},{64,32},{96,64},{128,96},{160,128},{192,160},{224,192},{256... | collective-permute-start | bytes 24584 | tf_op jit(solution)/shard_map/ppermute | solution.py:24
  45.7 5.3 collective-permute-start.9
  51.0 7.3 %collective-permute-start.10 = (f32[34,1,512]{2,0,1:T(8,128)S(1)}, f32[34,1,512]{2,0,1:T(8,128)S(1)}, u32[]{:S(2)}, u32[]{:S(2)}) collective-permute-start(f32[34,1,512]{2,0,1:T(8,128)S(1)} %get-tuple-element.607), channel_id=1, source_target_pairs={{1,0},{2,1},{3,2},{4,3},{5,4},{6,5},{7,6},{8,7},{9,8},{10,9},{11,1... | collective-permute-start | bytes 208904 | tf_op jit(solution)/shard_map/ppermute | solution.py:24
  53.0 6.6 %collective-permute-start.11 = (f32[34,1,512]{2,0,1:T(8,128)S(1)}, f32[34,1,512]{2,0,1:T(8,128)S(1)}, u32[]{:S(2)}, u32[]{:S(2)}) collective-permute-start(f32[34,1,512]{2,0,1:T(8,128)S(1)} %get-tuple-element.608), channel_id=1, source_target_pairs={{0,1},{1,2},{2,3},{3,4},{4,5},{5,6},{6,7},{7,8},{8,9},{9,10},{10,1... | collective-permute-start | bytes 208904 | tf_op jit(solution)/shard_map/ppermute | solution.py:23
  86.5 136.1 %all-gather.14.cloned.1.call-start = ((), (), s32[]{:S(2)}) async-start(), calls=%async_computation.2 | async-start | bytes 1114112 | tf_op jit(solution)/shard_map/all_gather | solution.py:31
  161.1 0.6 copy-start.3
  161.2 0.7 copy-start.2
  161.8 130.8 %all-gather.12.cloned.1.call-start = ((), (), s32[]{:S(2)}) async-start(), calls=%async_computation.1 | async-start | bytes 1114112 | tf_op jit(solution)/shard_map/all_gather | solution.py:31
  162.5 236.9 %all-gather.16.cloned.1.call-start = ((), (), s32[]{:S(2)}) async-start(), calls=%async_computation.3 | async-start | bytes 1114112 | tf_op jit(solution)/shard_map/all_gather | solution.py:31
  330.7 0.6 copy-start.1
  331.3 137.9 %all-gather.18.cloned.1.call-start = ((), (), s32[]{:S(2)}) async-start(), calls=%async_computation.4 | async-start | bytes 1114112 | tf_op jit(solution)/shard_map/all_gather | solution.py:31
  488.0 43.0 %copy-start = (f32[32,4,512]{2,1,0:T(4,128)S(1)}, f32[32,4,512]{2,1,0:T(4,128)}, u32[]{:S(2)}) copy-start(f32[32,4,512]{2,1,0:T(4,128)} %param.14) | copy-start | bytes 786436
  507.2 5.3 collective-permute-start.12
  508.5 4.8 collective-permute-start.13
  513.3 16.4 %collective-permute-start.14 = (f32[34,1,512]{2,0,1:T(8,128)S(1)}, f32[34,1,512]{2,0,1:T(8,128)S(1)}, u32[]{:S(2)}, u32[]{:S(2)}) collective-permute-start(f32[34,1,512]{2,0,1:T(8,128)S(1)} %get-tuple-element.605), channel_id=1, source_target_pairs={{1,0},{2,1},{3,2},{4,3},{5,4},{6,5},{7,6},{8,7},{9,8},{10,9},{11,1... | collective-permute-start | bytes 208904 | tf_op jit(solution)/shard_map/ppermute | solution.py:24
  526.5 4.5 collective-permute-start.15
  531.2 5.8 %collective-permute-start.16 = (f32[1,4,512]{2,0,1:T(1,128)S(1)}, f32[1,4,512]{2,0,1:T(1,128)S(1)}, u32[]{:S(2)}, u32[]{:S(2)}) collective-permute-start(f32[1,4,512]{2,0,1:T(1,128)S(1)} %get-tuple-element.614), channel_id=1, source_target_pairs={{32,0},{64,32},{96,64},{128,96},{160,128},{192,160},{224,192},{256... | collective-permute-start | bytes 24584 | tf_op jit(solution)/shard_map/ppermute | solution.py:24
  532.5 5.3 collective-permute-start.17
  537.9 7.3 %collective-permute-start.18 = (f32[34,1,512]{2,0,1:T(8,128)S(1)}, f32[34,1,512]{2,0,1:T(8,128)S(1)}, u32[]{:S(2)}, u32[]{:S(2)}) collective-permute-start(f32[34,1,512]{2,0,1:T(8,128)S(1)} %get-tuple-element.603), channel_id=1, source_target_pairs={{1,0},{2,1},{3,2},{4,3},{5,4},{6,5},{7,6},{8,7},{9,8},{10,9},{11,1... | collective-permute-start | bytes 208904 | tf_op jit(solution)/shard_map/ppermute | solution.py:24
  539.8 6.6 %collective-permute-start.19 = (f32[34,1,512]{2,0,1:T(8,128)S(1)}, f32[34,1,512]{2,0,1:T(8,128)S(1)}, u32[]{:S(2)}, u32[]{:S(2)}) collective-permute-start(f32[34,1,512]{2,0,1:T(8,128)S(1)} %get-tuple-element.604), channel_id=1, source_target_pairs={{0,1},{1,2},{2,3},{3,4},{4,5},{5,6},{6,7},{7,8},{8,9},{9,10},{10,1... | collective-permute-start | bytes 208904 | tf_op jit(solution)/shard_map/ppermute | solution.py:23
Sparse Core Ops, SparseCore 0:
  86.6 68.5 all-gather.9
  161.9 60.5 all-gather.13
  224.6 67.9 all-gather.11
  331.4 67.9 all-gather.15
  401.3 67.9 all-gather.17
where the time goes:
time: 562 us; the launch traced here: 554 us
  waiting for transfers between devices  345 us (61%)
  starting transfers between devices  77.3 us (14%)
  other arithmetic  64.6 us (11%)
  local copies, waits for them, and re-layouts  45 us (8%)
  between operations  13.7 us (2%)
  matrix products  7.03 us (1%)
    all_gather x4, waiting for transfers between devices, carried_in(): pieces = jax.tree.map(lambda part: lax.all_gather(part, axis), value)  266 us
    all_gather x1, waiting for transfers between devices, coarse_solve(): whole = lax.all_gather(coarse, 'xy', axis=1, tiled=True)  67.6 us
    ppermute x10, starting transfers between devices, with_halo(): before = lax.ppermute(last, axis, up)  42.2 us
    ppermute x10, starting transfers between devices, with_halo(): after = lax.ppermute(initial, axis, down)  34.8 us
    select_n x30, other arithmetic, step(): jnp.where(position < mine, new, old)  27 us
    add x16, other arithmetic, down_step(): return ((pivot * carry[0], value + pivot * carry[1]), None)  23.2 us
    reshape x1, local copies, waits for them, and re-layouts, body(): residual.reshape(height // 2, 2, width // 2, 2, depth_y // 2, 2)  18.1 us
    reshape x1, local copies, waits for them, and re-layouts, body(): field = field + lifted.reshape(height, width, depth_y)  12.7 us
  transfers between devices with their start and end apart: 25, of which 18 were waited for; matrix products, arithmetic and copies ran while one was open for 1% of the time, Pallas kernels for 0%

commit v1 on v0

v1 whole, which is shorter than its diff:
```python
import functools
import math

import jax
import jax.numpy as jnp
import numpy as np
from jax import lax
from jax.experimental import pallas as pl
from jax.experimental.pallas import tpu as pltpu
from jax.sharding import PartitionSpec as P

SCREEN = 64
OMEGA = 0.8
KAPPA = 1.0 / (SCREEN * SCREEN)
CW = 6.0 + KAPPA
HIGH = lax.Precision.HIGHEST
M = 8
CORNERS = ((-1, -1), (-1, 1), (1, -1), (1, 1))


def sine(count):
    idx = np.arange(1, count + 1, dtype=np.int64)
    turns = idx[:, None] * idx[None, :] % (2 * (count + 1))
    return math.sqrt(2.0 / (count + 1)) * np.sin(math.pi / (count + 1) * turns)


def eigen(count):
    return 2.0 - 2.0 * np.cos(math.pi / (count + 1) * np.arange(1, count + 1))


def tables(groups):
    nx, ny = 2 * groups, M * groups
    sx, sy = sine(nx), sine(ny)
    ty = np.repeat(sy, 2, axis=1)
    order = np.concatenate([np.arange(0, nx, 2), np.arange(1, nx, 2)])
    fx = 0.5 * np.concatenate([sx[order], sx[order]], axis=1)
    bx = np.zeros((groups, 8, 2 * nx))
    for d in range(groups):
        for e in range(4):
            x = 2 * d - 1 + e
            if 0 <= x < nx:
                bx[d, e, :nx] = sx[x]
                bx[d, 4 + e, nx:] = sx[x]
    diag = 2.0 + eigen(nx)[None, None, :] + eigen(ny).reshape(M, groups).T[:, :, None] + 4.0 * KAPPA
    theta = np.arccosh(0.5 * diag)
    theta = np.concatenate([theta, theta], axis=2)
    f = lambda t: np.asarray(t, np.float32)
    return f(ty), f(fx), f(bx.reshape(groups * 8, 2 * nx)), f(theta)


def kernel(
    gz, xy, src_hbm, pot_hbm, ty_hbm, fx_hbm, bx_hbm, th_hbm, out_ref,
    potv, srcv, ty, fx, bx, th, pa, pb, sv,
    xps, xpr, xss, xsr, zpr, zsr, cs, cr,
    xqs, xqr, zqr, ds, dr,
    rs, s1, r1, fz, wz, ztile, zr, vz, s2, r2, cc,
    ld, e1s, e1r, e2s, e2r, a1s, a1r, gs, gr, a2s, a2r,
):
    q, me = lax.axis_index("gz"), lax.axis_index("xy")
    planes, rows, ny = potv.shape
    half = 2 * xy

    loads = [
        pltpu.make_async_copy(pot_hbm, potv, ld.at[0]),
        pltpu.make_async_copy(src_hbm, srcv, ld.at[1]),
        pltpu.make_async_copy(ty_hbm, ty, ld.at[2]),
        pltpu.make_async_copy(fx_hbm, fx, ld.at[3]),
        pltpu.make_async_copy(bx_hbm, bx, ld.at[4]),
        pltpu.make_async_copy(th_hbm.at[me], th, ld.at[5]),
    ]
    for copy in loads:
        copy.start()

    def shifted(dz, dx):
        where = {}
        if dz:
            where["gz"] = lax.rem(q + dz + gz, gz)
        if dx:
            where["xy"] = lax.rem(me + dx + xy, xy)
        return where

    barrier = pltpu.get_barrier_semaphore()
    for dz, dx in CORNERS:
        pl.semaphore_signal(barrier, inc=1, device_id=shifted(dz, dx), device_id_type=pl.DeviceIdType.MESH)

    def greet_x(i, carry):
        pl.semaphore_signal(barrier, inc=1, device_id={"xy": lax.rem(me + i, xy)}, device_id_type=pl.DeviceIdType.MESH)
        return carry

    def greet_z(i, carry):
        pl.semaphore_signal(barrier, inc=1, device_id={"gz": lax.rem(q + i, gz)}, device_id_type=pl.DeviceIdType.MESH)
        return carry

    lax.fori_loop(1, xy, greet_x, 0)
    lax.fori_loop(1, gz, greet_z, 0)

    pa[...] = jnp.zeros_like(pa)
    sv[...] = jnp.zeros_like(sv)
    loads[0].wait()
    loads[1].wait()
    xps[0] = potv[:, 0:2, :]
    xps[1] = potv[:, 2:4, :]
    xss[0] = srcv[:, 0:1, :]
    xss[1] = srcv[:, 3:4, :]
    for c, (dz, dx) in enumerate(CORNERS):
        z, x = 0 if dz < 0 else planes - 1, 0 if dx < 0 else rows - 1
        cs[c] = potv[z, x : x + 1, :]
    pl.semaphore_wait(barrier, (xy - 1) + (gz - 1) + len(CORNERS))

    def remote(src, dst, send, recv, where):
        return pltpu.make_async_remote_copy(
            src_ref=src, dst_ref=dst, send_sem=send, recv_sem=recv,
            device_id=where, device_id_type=pl.DeviceIdType.MESH,
        )

    first = []
    for side, step in ((0, -1), (1, 1)):
        z = 0 if step < 0 else planes - 2
        z1 = 0 if step < 0 else planes - 1
        first.append(remote(xps.at[side], xpr.at[side], e1s.at[side], e1r.at[side], shifted(0, step)))
        first.append(remote(xss.at[side], xsr.at[side], e1s.at[2 + side], e1r.at[2 + side], shifted(0, step)))
        first.append(remote(potv.at[pl.ds(z, 2)], zpr.at[side], e1s.at[4 + side], e1r.at[4 + side], shifted(step, 0)))
        first.append(remote(srcv.at[pl.ds(z1, 1)], zsr.at[side], e1s.at[6 + side], e1r.at[6 + side], shifted(step, 0)))
    for c, (dz, dx) in enumerate(CORNERS):
        first.append(remote(cs.at[c], cr.at[c], e1s.at[8 + c], e1r.at[8 + c], shifted(dz, dx)))
    for copy in first:
        copy.start()

    pa[2 : planes + 2, 2:6, :] = potv[...]
    sv[1 : planes + 1, 2:6, :] = srcv[...]
    sub = lax.broadcasted_iota(jnp.int32, (8, ny), 0)
    lane = lax.broadcasted_iota(jnp.int32, (8, ny), 1)
    inside = jnp.logical_and(
        jnp.logical_or(sub >= 2, me > 0), jnp.logical_or(sub < 6, me < xy - 1)
    )
    low, high = (q > 0).astype(jnp.float32), (q < gz - 1).astype(jnp.float32)
    near, far = (me > 0).astype(jnp.float32), (me < xy - 1).astype(jnp.float32)

    def corners_in(corner):
        for c, (dz, dx) in enumerate(CORNERS):
            plane, edge = (planes + 2, high) if dz < 0 else (1, low)
            row, side = (6, far) if dx < 0 else (1, near)
            pa[plane, row : row + 1, :] = corner[c] * (edge * side)

    for copy in first:
        copy.wait()
    pa[2 : planes + 2, 0:2, :] = xpr[1] * near
    pa[2 : planes + 2, 6:8, :] = xpr[0] * far
    pa[0:2, 2:6, :] = zpr[1] * low
    pa[planes + 2 : planes + 4, 2:6, :] = zpr[0] * high
    sv[1 : planes + 1, 1:2, :] = xsr[1] * near
    sv[1 : planes + 1, 6:7, :] = xsr[0] * far
    sv[0:1, 2:6, :] = zsr[1] * low
    sv[planes + 1 : planes + 2, 2:6, :] = zsr[0] * high
    corners_in(cr)

    def neighbours(ref, i):
        v = ref[i]
        total = ref[i - 1] + ref[i + 1]
        total = total + pltpu.roll(v, 1, 0) + pltpu.roll(v, 7, 0)
        total = total + jnp.where(lane == 0, 0.0, pltpu.roll(v, 1, 1))
        total = total + jnp.where(lane == ny - 1, 0.0, pltpu.roll(v, ny - 1, 1))
        return v, total

    def relax(ref, i):
        v, total = neighbours(ref, i)
        return (1.0 - OMEGA) * v + (OMEGA / CW) * (sv[i - 1] + total)

    def wide_sweep():
        def step(i, carry):
            pb[i] = jnp.where(inside, relax(pa, i), 0.0)
            return carry

        lax.fori_loop(1, planes + 3, step, 0, unroll=2)
        pb[1] = pb[1] * low
        pb[planes + 2] = pb[planes + 2] * high

    wide_sweep()

    def own_sweep(i, carry):
        pa[i] = relax(pb, i)
        return carry

    lax.fori_loop(2, planes + 2, own_sweep, 0, unroll=2)

    xqs[0] = pa[2 : planes + 2, 2:4, :]
    xqs[1] = pa[2 : planes + 2, 4:6, :]
    for c, (dz, dx) in enumerate(CORNERS):
        z, x = 2 if dz < 0 else planes + 1, 2 if dx < 0 else 5
        ds[c] = pa[z, x : x + 1, :]
    second = []
    for side, step in ((0, -1), (1, 1)):
        z = 2 if step < 0 else planes
        second.append(remote(xqs.at[side], xqr.at[side], e2s.at[side], e2r.at[side], shifted(0, step)))
        second.append(remote(pa.at[pl.ds(z, 2)], zqr.at[side], e2s.at[2 + side], e2r.at[2 + side], shifted(step, 0)))
    for c, (dz, dx) in enumerate(CORNERS):
        second.append(remote(ds.at[c], dr.at[c], e2s.at[4 + c], e2r.at[4 + c], shifted(dz, dx)))
    for copy in second:
        copy.start()
    for copy in second:
        copy.wait()
    pa[2 : planes + 2, 0:2, :] = xqr[1] * near
    pa[2 : planes + 2, 6:8, :] = xqr[0] * far
    pa[0:2, 2:6, :] = zqr[1, :, 2:6, :] * low
    pa[planes + 2 : planes + 4, 2:6, :] = zqr[0, :, 2:6, :] * high
    corners_in(dr)

    def residual(i):
        v, total = neighbours(pa, i)
        return sv[i - 1] - CW * v + total

    def coarsen(z, carry):
        rs[z] = residual(2 * z + 2) + residual(2 * z + 3)
        return carry

    coarse = planes // 2
    lax.fori_loop(0, coarse, coarsen, 0)
    for copy in loads[2:]:
        copy.wait()
    wide = coarse * 8
    spec = lax.dot_general(
        ty[...], rs[...].reshape(wide, ny), (((1,), (1,)), ((), ())),
        precision=HIGH, preferred_element_type=jnp.float32,
    )
    spec = spec + pltpu.roll(spec, wide - 1, 1)
    slot = lax.broadcasted_iota(jnp.int32, (xy, wide), 1) % 8
    for xx in range(2):
        packed = jnp.zeros((xy, wide), jnp.float32)
        for m in range(M):
            piece = spec[m * xy : (m + 1) * xy, :]
            shift = (m - 2 - 2 * xx) % wide
            piece = pltpu.roll(piece, shift, 1) if shift else piece
            packed = jnp.where(slot == m, piece, packed)
        s1[:, xx : xx + 1, :] = packed.reshape(xy, 1, wide)

    def everyone(axis, size, mine, src_of, dst, send, recv):
        def copy_to(i):
            to = lax.rem(mine + i, size)
            return remote(src_of(to), dst.at[mine], send.at[to], recv.at[mine], {axis: to})

        def copy_from(i):
            to = lax.rem(mine + i, size)
            return remote(src_of(to), dst.at[to], send.at[to], recv.at[to], {axis: to})

        def go(i, carry):
            copy_to(i).start()
            return carry

        def done(i, carry):
            copy_from(i).wait()
            return carry

        lax.fori_loop(1, size, go, 0)
        dst[mine] = src_of(mine)[...]
        lax.fori_loop(1, size, done, 0)

    everyone("xy", xy, me, lambda to: s1.at[to], r1, a1s, a1r)
    gathered = jnp.concatenate([r1[:, 0:1, :].reshape(xy, wide), r1[:, 1:2, :].reshape(xy, wide)], axis=0)
    fz[...] = lax.dot_general(
        gathered, fx[...], (((0,), (0,)), ((), ())),
        precision=HIGH, preferred_element_type=jnp.float32,
    ).reshape(coarse, M, 2 * half)

    up = lax.broadcasted_iota(jnp.int32, (M, 2 * half), 1) < half
    theta = th[...]
    decay = jnp.exp(-theta)
    state = jnp.zeros((M, 2 * half), jnp.float32)
    for t in range(coarse):
        state = decay * state + jnp.where(up, fz[t], fz[coarse - 1 - t])
        wz[t] = state
    ztile[...] = state
    everyone("gz", gz, q, lambda to: ztile, zr, gs, gr)
    block = jnp.exp(-float(coarse) * theta)
    total = jnp.zeros((M, 2 * half), jnp.float32)
    inflow = jnp.zeros((M, 2 * half), jnp.float32)
    steps_in = jnp.where(up, q, gz - 1 - q)
    for t in range(gz):
        inflow = jnp.where(steps_in == t, total, inflow)
        total = block * total + jnp.where(up, zr[t], zr[gz - 1 - t])
    span = float(coarse * gz + 1)
    image = pltpu.roll(total, half, 1) - jnp.exp(-span * theta) * total
    image = image * jnp.exp(-theta * (float(coarse) * steps_in.astype(jnp.float32) + 1.0))
    inflow = inflow - image / (1.0 - jnp.exp(-2.0 * span * theta))
    scale = 1.0 / (jnp.exp(theta) - decay)
    power = decay
    for t in range(coarse):
        wz[t] = wz[t] + power * inflow
        power = power * decay
    last = decay * wz[coarse - 1]
    beyond = scale * (last + pltpu.roll(inflow, half, 1))
    above, below = beyond * high, beyond * low
    above = pltpu.roll(above, half, 1)
    for z in range(coarse):
        value = scale * (wz[z] + pltpu.roll(wz[coarse - 1 - z], half, 1) - fz[z])
        ring = below if z == 0 else above if z == 1 else 0.0
        vz[z] = jnp.where(up, value, ring)
    s2[...] = lax.dot_general(
        bx[...], vz[...].reshape(wide, 2 * half), (((1,), (1,)), ((), ())),
        precision=HIGH, preferred_element_type=jnp.float32,
    ).reshape(xy, 8, wide)
    everyone("xy", xy, me, lambda to: s2.at[to], r2, a2s, a2r)

    def spread(base):
        parts = [r2[:, base + e : base + e + 1, :].reshape(xy, wide) for e in range(4)]
        modes = []
        for m in range(M):
            mixed = jnp.zeros((xy, wide), jnp.float32)
            for e in range(4):
                shift = (2 * e - m) % wide
                piece = pltpu.roll(parts[e], shift, 1) if shift else parts[e]
                mixed = jnp.where(slot == 2 * e, piece, mixed)
            modes.append(mixed + pltpu.roll(mixed, 1, 1))
        return jnp.concatenate(modes, axis=0)

    turned = jnp.concatenate([spread(0).T, spread(4).T[:16]], axis=0)
    cc[...] = jnp.dot(
        turned, ty[...], precision=HIGH, preferred_element_type=jnp.float32
    ).reshape(coarse + 2, 8, ny)

    def lift(z, carry):
        fix = cc[z]
        pa[2 * z + 2] = pa[2 * z + 2] + fix
        pa[2 * z + 3] = pa[2 * z + 3] + fix
        return carry

    lax.fori_loop(0, coarse, lift, 0)
    for i, z in ((0, coarse), (1, coarse), (planes + 2, coarse + 1), (planes + 3, coarse + 1)):
        pa[i] = pa[i] + cc[z]
    wide_sweep()

    def last_sweep(i, carry):
        out_ref[i - 2] = relax(pb, i)[2:6, :]
        return carry

    lax.fori_loop(2, planes + 2, last_sweep, 0, unroll=2)


def body(gz, xy, consts, source, potential):
    planes, rows, ny = source.shape
    coarse = planes // 2
    wide, two = coarse * 8, 4 * xy
    f32 = jnp.float32
    vm = lambda *shape: pltpu.VMEM(shape, f32)
    dma = lambda n: pltpu.SemaphoreType.DMA((n,))
    scratch = [
        vm(planes, rows, ny), vm(planes, rows, ny), vm(M * xy, ny), vm(2 * xy, two), vm(8 * xy, two), vm(M, two),
        vm(planes + 4, 8, ny), vm(planes + 4, 8, ny), vm(planes + 2, 8, ny),
        vm(2, planes, 2, ny), vm(2, planes, 2, ny), vm(2, planes, 1, ny), vm(2, planes, 1, ny),
        vm(2, 2, rows, ny), vm(2, 1, rows, ny), vm(4, 1, ny), vm(4, 1, ny),
        vm(2, planes, 2, ny), vm(2, planes, 2, ny), vm(2, 2, 8, ny), vm(4, 1, ny), vm(4, 1, ny),
        vm(coarse, 8, ny), vm(xy, 2, wide), vm(xy, 2, wide), vm(coarse, M, two), vm(coarse, M, two),
        vm(M, two), vm(gz, M, two), vm(coarse, M, two), vm(xy, 8, wide), vm(xy, 8, wide), vm(coarse + 2, 8, ny),
        dma(6), dma(12), dma(12), dma(8), dma(8), dma(xy), dma(xy), dma(gz), dma(gz), dma(xy), dma(xy),
    ]
    hbm = pl.BlockSpec(memory_space=pl.ANY)
    return pl.pallas_call(
        functools.partial(kernel, gz, xy),
        out_shape=jax.ShapeDtypeStruct(source.shape, f32),
        in_specs=[hbm] * 6,
        out_specs=pl.BlockSpec(memory_space=pltpu.VMEM),
        scratch_shapes=scratch,
        compiler_params=pltpu.CompilerParams(collective_id=0, has_side_effects=True),
        name="vcycle",
    )(source, potential, *[jnp.asarray(c) for c in consts])


def solution(mesh):
    gz, xy = mesh.shape["gz"], mesh.shape["xy"]
    consts = tables(xy)
    placed = (P("gz", "xy", None), P("gz", "xy", None))
    return jax.shard_map(
        functools.partial(body, gz, xy, consts), mesh=mesh, in_specs=placed,
        out_specs=P("gz", "xy", None), check_vma=False,
    )
```

time: 562 us -> 60.2 us (0.11); the launches traced: 554 us -> 60 us
  waiting for transfers between devices: 345 us -> 0 us
  starting transfers between devices: 77.3 us -> 0 us
  other arithmetic: 64.6 us -> 0 us
  Pallas kernels: 0 us -> 58.4 us
  local copies, waits for them, and re-layouts: 45 us -> 1.67 us
  between operations: 13.7 us -> 0.01 us
  matrix products: 7.03 us -> 0 us
    all_gather x5 -> x0, waiting for transfers between devices: 333 us -> none  [the longest x4 266 us: carried_in(): pieces = jax.tree.map(lambda part: lax.all_gather(part, axis), value)]
    ppermute x20 -> x0, starting transfers between devices: 77 us -> none  [the longest x10 42.2 us: with_halo(): before = lax.ppermute(last, axis, up)]
    pallas_call x0 -> x1, Pallas kernels: none -> 58.4 us  [body(): pl.pallas_call(functools.partial(kernel, gz, xy), out_shape=jax.ShapeDtyp...]
    reshape x2 -> x0, local copies, waits for them, and re-layouts: 30.8 us -> none  [the longest x1 18.1 us: body(): residual.reshape(height // 2, 2, width // 2, 2, depth_y // 2, 2)]
    select_n x30 -> x0, other arithmetic: 27 us -> none  [step(): jnp.where(position < mine, new, old)]
    add x24 -> x0, other arithmetic: 26.3 us -> none  [the longest x16 23.2 us: down_step(): return ((pivot * carry[0], value + pivot * carry[1]), None)]
    ppermute x20 -> x0, waiting for transfers between devices: 10.4 us -> none  [the longest x10 9.64 us: with_halo(): before = lax.ppermute(last, axis, up)]
    dot_general x4 -> x0, matrix products: 7.03 us -> none  [the longest x1 3.75 us: coarse_solve(): jnp.dot(whole.reshape(-1, cols), table_y, precision=HIGH)]
  transfers between devices with their start and end apart: 25 -> 0, of which waited for: 18 -> 0; matrix products, arithmetic and copies ran while one was open for 1% -> 0% of each run, Pallas kernels for 0% -> 0%
where the time goes in v1:
time: 60.2 us; the launch traced here: 60 us
  Pallas kernels  58.4 us (97%)
  local copies, waits for them, and re-layouts  1.67 us (3%)
    pallas_call x1, Pallas kernels, body(): pl.pallas_call(functools.partial(kernel, gz, xy), out_shape=jax.ShapeDtyp...  58.4 us
    unnamed x1, local copies, waits for them, and re-layouts  1.67 us

profile of v1, /device:TPU:1, one launch (start us, length us, event | category | flops | bytes accessed | tf_op | source)
XLA Modules:
  0.0 60.0 jit_solution(10405192746473773447)
XLA Ops:
  0.0 58.4 %vcycle.1 = f32[32,4,512]{2,1,0:T(4,128)} custom-call(f32[32,4,512]{2,1,0:T(4,128)} %src_hbm.1, f32[32,4,512]{2,1,0:T(4,128)} %pot_hbm.1, f32[256,512]{1,0:T(8,128)} %constant.8.clone.ty_hbm, f32[64,128]{1,0:T(8,128)} %constant.9.clone.fx_hbm, f32[256,128]{1,0:T(8,128)} %constant.10.clone.bx_hbm, f32[32,8,128]{2,1,0:T(8,128)} %constant.11.clone.th_hbm), custom_call_target="tpu_custom_call" | custom-call | tf_op jit(solution)/shard_map/vcycle/pallas_call | solution.py:356
  58.4 1.7 %copy.8 = f32[32,4,512]{2,1,0:T(4,128)} copy(f32[32,4,512]{2,1,0:T(4,128)} %vcycle.1) | data formatting | bytes 524288

commit v2 on v1

--- a/solution.py
+++ b/solution.py
@@ -51,14 +51,15 @@
 def kernel(
     gz, xy, src_hbm, pot_hbm, ty_hbm, fx_hbm, bx_hbm, th_hbm, out_ref,
     potv, srcv, ty, fx, bx, th, pa, pb, sv,
-    xps, xpr, xss, xsr, zpr, zsr, cs, cr,
+    xps, xpr, xts, xtr, xss, xsr, zpr, zsr, cs, cr,
     xqs, xqr, zqr, ds, dr,
     rs, s1, r1, fz, wz, ztile, zr, vz, s2, r2, cc,
-    ld, e1s, e1r, e2s, e2r, a1s, a1r, gs, gr, a2s, a2r,
+    ld, e1s, e1r, e2s, e2r, a1s, a1r, gs, gr, a2s, a2r, known_x, known_z,
 ):
     q, me = lax.axis_index("gz"), lax.axis_index("xy")
     planes, rows, ny = potv.shape
     half = 2 * xy
+    top = planes + 3
 
     loads = [
         pltpu.make_async_copy(pot_hbm, potv, ld.at[0]),
@@ -79,33 +80,71 @@
             where["xy"] = lax.rem(me + dx + xy, xy)
         return where
 
+    def tell(sem, where):
+        pl.semaphore_signal(sem, inc=1, device_id=where, device_id_type=pl.DeviceIdType.MESH)
+
     barrier = pltpu.get_barrier_semaphore()
-    for dz, dx in CORNERS:
-        pl.semaphore_signal(barrier, inc=1, device_id=shifted(dz, dx), device_id_type=pl.DeviceIdType.MESH)
-
-    def greet_x(i, carry):
-        pl.semaphore_signal(barrier, inc=1, device_id={"xy": lax.rem(me + i, xy)}, device_id_type=pl.DeviceIdType.MESH)
-        return carry
-
-    def greet_z(i, carry):
-        pl.semaphore_signal(barrier, inc=1, device_id={"gz": lax.rem(q + i, gz)}, device_id_type=pl.DeviceIdType.MESH)
-        return carry
-
-    lax.fori_loop(1, xy, greet_x, 0)
-    lax.fori_loop(1, gz, greet_z, 0)
+    for dz, dx in CORNERS + ((-1, 0), (1, 0), (0, -1), (0, 1)):
+        tell(barrier, shifted(dz, dx))
 
     pa[...] = jnp.zeros_like(pa)
     sv[...] = jnp.zeros_like(sv)
+    for side in range(2):
+        xtr[side, 0:2] = jnp.zeros((2, 1, ny), jnp.float32)
+        xtr[side, planes + 2 : planes + 4] = jnp.zeros((2, 1, ny), jnp.float32)
     loads[0].wait()
     loads[1].wait()
     xps[0] = potv[:, 0:2, :]
     xps[1] = potv[:, 2:4, :]
-    xss[0] = srcv[:, 0:1, :]
-    xss[1] = srcv[:, 3:4, :]
-    for c, (dz, dx) in enumerate(CORNERS):
-        z, x = 0 if dz < 0 else planes - 1, 0 if dx < 0 else rows - 1
-        cs[c] = potv[z, x : x + 1, :]
-    pl.semaphore_wait(barrier, (xy - 1) + (gz - 1) + len(CORNERS))
+    xts[0] = potv[:, 2:3, :]
+    xts[1] = potv[:, 1:2, :]
+    xss[0] = srcv[:, 0:2, :]
+    xss[1] = srcv[:, 2:4, :]
+    for c, (dz, dx) in enumerate(CORNERS):
+        z0, z1 = (0, 1) if dz < 0 else (planes - 1, planes - 2)
+        x0, x1 = (0, 1) if dx < 0 else (rows - 1, rows - 2)
+        cs[c, 0:1] = potv[z0, x0 : x0 + 1, :]
+        cs[c, 1:2] = potv[z0, x1 : x1 + 1, :]
+        cs[c, 2:3] = potv[z1, x0 : x0 + 1, :]
+        cs[c, 3:4] = srcv[z0, x0 : x0 + 1, :]
+    pl.semaphore_wait(barrier, 8)
+
+    def round_of(level):
+        for axis, size, dim, known in (("xy", xy, 1, known_x), ("gz", gz, 0, known_z)):
+            reach = 2**level
+            if level and reach // 2 < size // 2:
+                pl.semaphore_wait(known.at[level - 1], 2)
+            if reach < size // 2:
+                for way in (-reach, reach):
+                    tell(known.at[level], shifted(way, 0) if dim == 0 else shifted(0, way))
+
+    round_of(0)
+
+    class Exchange:
+        def __init__(self, send, recv):
+            self.send, self.recv, self.copies = send, recv, []
+
+        def add(self, src, dst, dz, dx):
+            slot = len(self.copies)
+            copy = remote(src, dst, self.send.at[slot], self.recv.at[slot], shifted(dz, dx))
+            self.copies.append((copy, exists(dz, dx), exists(-dz, -dx)))
+
+        def start(self):
+            for copy, there, unused in self.copies:
+                pl.when(there)(copy.start)
+
+        def wait(self):
+            for copy, there, back in self.copies:
+                pl.when(back)(copy.wait_recv)
+                pl.when(there)(copy.wait_send)
+
+    def exists(dz, dx):
+        there = None
+        for step, mine, size in ((dz, q, gz), (dx, me, xy)):
+            if step:
+                ok = mine > 0 if step < 0 else mine < size - 1
+                there = ok if there is None else jnp.logical_and(there, ok)
+        return there
 
     def remote(src, dst, send, recv, where):
         return pltpu.make_async_remote_copy(
@@ -113,104 +152,101 @@
             device_id=where, device_id_type=pl.DeviceIdType.MESH,
         )
 
-    first = []
+    first = Exchange(e1s, e1r)
     for side, step in ((0, -1), (1, 1)):
-        z = 0 if step < 0 else planes - 2
-        z1 = 0 if step < 0 else planes - 1
-        first.append(remote(xps.at[side], xpr.at[side], e1s.at[side], e1r.at[side], shifted(0, step)))
-        first.append(remote(xss.at[side], xsr.at[side], e1s.at[2 + side], e1r.at[2 + side], shifted(0, step)))
-        first.append(remote(potv.at[pl.ds(z, 2)], zpr.at[side], e1s.at[4 + side], e1r.at[4 + side], shifted(step, 0)))
-        first.append(remote(srcv.at[pl.ds(z1, 1)], zsr.at[side], e1s.at[6 + side], e1r.at[6 + side], shifted(step, 0)))
-    for c, (dz, dx) in enumerate(CORNERS):
-        first.append(remote(cs.at[c], cr.at[c], e1s.at[8 + c], e1r.at[8 + c], shifted(dz, dx)))
-    for copy in first:
-        copy.start()
-
-    pa[2 : planes + 2, 2:6, :] = potv[...]
-    sv[1 : planes + 1, 2:6, :] = srcv[...]
+        first.add(xps.at[side], xpr.at[side], 0, step)
+        first.add(xts.at[side], xtr.at[side, pl.ds(2, planes)], 0, step)
+        first.add(xss.at[side], xsr.at[side], 0, step)
+        first.add(potv.at[pl.ds(0 if step < 0 else planes - 3, 3)], zpr.at[side], step, 0)
+        first.add(srcv.at[pl.ds(0 if step < 0 else planes - 2, 2)], zsr.at[side], step, 0)
+    for c, (dz, dx) in enumerate(CORNERS):
+        first.add(cs.at[c], cr.at[c], dz, dx)
+    first.start()
+
+    pa[3:top, 2:6, :] = potv[...]
+    sv[2 : planes + 2, 2:6, :] = srcv[...]
     sub = lax.broadcasted_iota(jnp.int32, (8, ny), 0)
     lane = lax.broadcasted_iota(jnp.int32, (8, ny), 1)
     inside = jnp.logical_and(
         jnp.logical_or(sub >= 2, me > 0), jnp.logical_or(sub < 6, me < xy - 1)
     )
-    low, high = (q > 0).astype(jnp.float32), (q < gz - 1).astype(jnp.float32)
-    near, far = (me > 0).astype(jnp.float32), (me < xy - 1).astype(jnp.float32)
-
-    def corners_in(corner):
-        for c, (dz, dx) in enumerate(CORNERS):
-            plane, edge = (planes + 2, high) if dz < 0 else (1, low)
-            row, side = (6, far) if dx < 0 else (1, near)
-            pa[plane, row : row + 1, :] = corner[c] * (edge * side)
-
-    for copy in first:
-        copy.wait()
-    pa[2 : planes + 2, 0:2, :] = xpr[1] * near
-    pa[2 : planes + 2, 6:8, :] = xpr[0] * far
-    pa[0:2, 2:6, :] = zpr[1] * low
-    pa[planes + 2 : planes + 4, 2:6, :] = zpr[0] * high
-    sv[1 : planes + 1, 1:2, :] = xsr[1] * near
-    sv[1 : planes + 1, 6:7, :] = xsr[0] * far
-    sv[0:1, 2:6, :] = zsr[1] * low
-    sv[planes + 1 : planes + 2, 2:6, :] = zsr[0] * high
-    corners_in(cr)
-
-    def neighbours(ref, i):
+    has_low, has_high, has_near, has_far = q > 0, q < gz - 1, me > 0, me < xy - 1
+
+    def corner_places(dz, dx):
+        z0, z1 = (top, top + 1) if dz < 0 else (2, 1)
+        x0, x1 = (6, 7) if dx < 0 else (1, 0)
+        return z0, z1, x0, x1, exists(-dz, -dx)
+
+    first.wait()
+    round_of(1)
+    pa[3:top, 0:2, :] = jnp.where(has_near, xpr[1], 0.0)
+    pa[3:top, 6:8, :] = jnp.where(has_far, xpr[0], 0.0)
+    pa[0:3, 2:6, :] = jnp.where(has_low, zpr[1], 0.0)
+    pa[top : top + 3, 2:6, :] = jnp.where(has_high, zpr[0], 0.0)
+    sv[2 : planes + 2, 0:2, :] = jnp.where(has_near, xsr[1], 0.0)
+    sv[2 : planes + 2, 6:8, :] = jnp.where(has_far, xsr[0], 0.0)
+    sv[0:2, 2:6, :] = jnp.where(has_low, zsr[1], 0.0)
+    sv[planes + 2 : planes + 4, 2:6, :] = jnp.where(has_high, zsr[0], 0.0)
+    for c, (dz, dx) in enumerate(CORNERS):
+        z0, z1, x0, x1, there = corner_places(dz, dx)
+        corner = jnp.where(there, cr[c], 0.0)
+        pa[z0, x0 : x0 + 1, :] = corner[0:1]
+        pa[z0, x1 : x1 + 1, :] = corner[1:2]
+        pa[z1, x0 : x0 + 1, :] = corner[2:3]
+        sv[z0 - 1, x0 : x0 + 1, :] = corner[3:4]
+
+    def neighbours(ref, i, ends=None):
         v = ref[i]
         total = ref[i - 1] + ref[i + 1]
-        total = total + pltpu.roll(v, 1, 0) + pltpu.roll(v, 7, 0)
+        back, forth = pltpu.roll(v, 1, 0), pltpu.roll(v, 7, 0)
+        if ends is not None:
+            back, forth = jnp.where(sub == 0, ends[0], back), jnp.where(sub == 7, ends[1], forth)
+        total = total + back + forth
         total = total + jnp.where(lane == 0, 0.0, pltpu.roll(v, 1, 1))
         total = total + jnp.where(lane == ny - 1, 0.0, pltpu.roll(v, ny - 1, 1))
         return v, total
 
-    def relax(ref, i):
-        v, total = neighbours(ref, i)
+    def relax(ref, i, ends=None):
+        v, total = neighbours(ref, i, ends)
         return (1.0 - OMEGA) * v + (OMEGA / CW) * (sv[i - 1] + total)
 
-    def wide_sweep():
+    def sweep(src, dst, ring, ended=False):
         def step(i, carry):
-            pb[i] = jnp.where(inside, relax(pa, i), 0.0)
+            ends = None
+            if ended:
+                ends = [jnp.where(there, xtr[side, i - 1], 0.0) for there, side in ((has_near, 1), (has_far, 0))]
+            dst[i] = jnp.where(inside, relax(src, i, ends), 0.0)
             return carry
 
-        lax.fori_loop(1, planes + 3, step, 0, unroll=2)
-        pb[1] = pb[1] * low
-        pb[planes + 2] = pb[planes + 2] * high
-
-    wide_sweep()
-
-    def own_sweep(i, carry):
-        pa[i] = relax(pb, i)
-        return carry
-
-    lax.fori_loop(2, planes + 2, own_sweep, 0, unroll=2)
-
-    xqs[0] = pa[2 : planes + 2, 2:4, :]
-    xqs[1] = pa[2 : planes + 2, 4:6, :]
-    for c, (dz, dx) in enumerate(CORNERS):
-        z, x = 2 if dz < 0 else planes + 1, 2 if dx < 0 else 5
+        lax.fori_loop(3 - ring, top + ring, step, 0, unroll=2)
+        for i in range(ring):
+            dst[2 - i] = jnp.where(has_low, dst[2 - i], 0.0)
+            dst[top + i] = jnp.where(has_high, dst[top + i], 0.0)
+
+    sweep(pa, pb, 2, True)
+    round_of(2)
+    sweep(pb, pa, 1)
+
+    xqs[0] = pa[3:top, 2:4, :]
+    xqs[1] = pa[3:top, 4:6, :]
+    for c, (dz, dx) in enumerate(CORNERS):
+        z, x = 3 if dz < 0 else top - 1, 2 if dx < 0 else 5
         ds[c] = pa[z, x : x + 1, :]
-    second = []
+    second = Exchange(e2s, e2r)
     for side, step in ((0, -1), (1, 1)):
-        z = 2 if step < 0 else planes
-        second.append(remote(xqs.at[side], xqr.at[side], e2s.at[side], e2r.at[side], shifted(0, step)))
-        second.append(remote(pa.at[pl.ds(z, 2)], zqr.at[side], e2s.at[2 + side], e2r.at[2 + side], shifted(step, 0)))
-    for c, (dz, dx) in enumerate(CORNERS):
-        second.append(remote(ds.at[c], dr.at[c], e2s.at[4 + c], e2r.at[4 + c], shifted(dz, dx)))
-    for copy in second:
-        copy.start()
-    for copy in second:
-        copy.wait()
-    pa[2 : planes + 2, 0:2, :] = xqr[1] * near
-    pa[2 : planes + 2, 6:8, :] = xqr[0] * far
-    pa[0:2, 2:6, :] = zqr[1, :, 2:6, :] * low
-    pa[planes + 2 : planes + 4, 2:6, :] = zqr[0, :, 2:6, :] * high
-    corners_in(dr)
+        second.add(xqs.at[side], xqr.at[side], 0, step)
+        second.add(pa.at[pl.ds(3 if step < 0 else top - 2, 2)], zqr.at[side], step, 0)
+    for c, (dz, dx) in enumerate(CORNERS):
+        second.add(ds.at[c], dr.at[c], dz, dx)
+    second.start()
+    round_of(3)
 
     def residual(i):
         v, total = neighbours(pa, i)
         return sv[i - 1] - CW * v + total
 
     def coarsen(z, carry):
-        rs[z] = residual(2 * z + 2) + residual(2 * z + 3)
+        rs[z] = residual(2 * z + 3) + residual(2 * z + 4)
         return carry
 
     coarse = planes // 2
@@ -254,6 +290,7 @@
         dst[mine] = src_of(mine)[...]
         lax.fori_loop(1, size, done, 0)
 
+    round_of(4)
     everyone("xy", xy, me, lambda to: s1.at[to], r1, a1s, a1r)
     gathered = jnp.concatenate([r1[:, 0:1, :].reshape(xy, wide), r1[:, 1:2, :].reshape(xy, wide)], axis=0)
     fz[...] = lax.dot_general(
@@ -288,7 +325,7 @@
         power = power * decay
     last = decay * wz[coarse - 1]
     beyond = scale * (last + pltpu.roll(inflow, half, 1))
-    above, below = beyond * high, beyond * low
+    above, below = jnp.where(has_high, beyond, 0.0), jnp.where(has_low, beyond, 0.0)
     above = pltpu.roll(above, half, 1)
     for z in range(coarse):
         value = scale * (wz[z] + pltpu.roll(wz[coarse - 1 - z], half, 1) - fz[z])
@@ -317,22 +354,31 @@
         turned, ty[...], precision=HIGH, preferred_element_type=jnp.float32
     ).reshape(coarse + 2, 8, ny)
 
+    second.wait()
+    pa[3:top, 0:2, :] = jnp.where(has_near, xqr[1], 0.0)
+    pa[3:top, 6:8, :] = jnp.where(has_far, xqr[0], 0.0)
+    pa[1:3, 2:6, :] = jnp.where(has_low, zqr[1, :, 2:6, :], 0.0)
+    pa[top : top + 2, 2:6, :] = jnp.where(has_high, zqr[0, :, 2:6, :], 0.0)
+    for c, (dz, dx) in enumerate(CORNERS):
+        z0, z1, x0, x1, there = corner_places(dz, dx)
+        pa[z0, x0 : x0 + 1, :] = jnp.where(there, dr[c], 0.0)
+
     def lift(z, carry):
         fix = cc[z]
-        pa[2 * z + 2] = pa[2 * z + 2] + fix
         pa[2 * z + 3] = pa[2 * z + 3] + fix
+        pa[2 * z + 4] = pa[2 * z + 4] + fix
         return carry
 
     lax.fori_loop(0, coarse, lift, 0)
-    for i, z in ((0, coarse), (1, coarse), (planes + 2, coarse + 1), (planes + 3, coarse + 1)):
+    for i, z in ((1, coarse), (2, coarse), (top, coarse + 1), (top + 1, coarse + 1)):
         pa[i] = pa[i] + cc[z]
-    wide_sweep()
+    sweep(pa, pb, 1)
 
     def last_sweep(i, carry):
-        out_ref[i - 2] = relax(pb, i)[2:6, :]
+        out_ref[i - 3] = relax(pb, i)[2:6, :]
         return carry
 
-    lax.fori_loop(2, planes + 2, last_sweep, 0, unroll=2)
+    lax.fori_loop(3, top, last_sweep, 0, unroll=2)
 
 
 def body(gz, xy, consts, source, potential):
@@ -344,13 +390,15 @@
     dma = lambda n: pltpu.SemaphoreType.DMA((n,))
     scratch = [
         vm(planes, rows, ny), vm(planes, rows, ny), vm(M * xy, ny), vm(2 * xy, two), vm(8 * xy, two), vm(M, two),
-        vm(planes + 4, 8, ny), vm(planes + 4, 8, ny), vm(planes + 2, 8, ny),
-        vm(2, planes, 2, ny), vm(2, planes, 2, ny), vm(2, planes, 1, ny), vm(2, planes, 1, ny),
-        vm(2, 2, rows, ny), vm(2, 1, rows, ny), vm(4, 1, ny), vm(4, 1, ny),
+        vm(planes + 6, 8, ny), vm(planes + 6, 8, ny), vm(planes + 4, 8, ny),
+        vm(2, planes, 2, ny), vm(2, planes, 2, ny), vm(2, planes, 1, ny), vm(2, planes + 4, 1, ny),
+        vm(2, planes, 2, ny), vm(2, planes, 2, ny),
+        vm(2, 3, rows, ny), vm(2, 2, rows, ny), vm(4, 4, ny), vm(4, 4, ny),
         vm(2, planes, 2, ny), vm(2, planes, 2, ny), vm(2, 2, 8, ny), vm(4, 1, ny), vm(4, 1, ny),
         vm(coarse, 8, ny), vm(xy, 2, wide), vm(xy, 2, wide), vm(coarse, M, two), vm(coarse, M, two),
         vm(M, two), vm(gz, M, two), vm(coarse, M, two), vm(xy, 8, wide), vm(xy, 8, wide), vm(coarse + 2, 8, ny),
-        dma(6), dma(12), dma(12), dma(8), dma(8), dma(xy), dma(xy), dma(gz), dma(gz), dma(xy), dma(xy),
+        dma(6), dma(14), dma(14), dma(8), dma(8), dma(xy), dma(xy), dma(gz), dma(gz), dma(xy), dma(xy),
+        pltpu.SemaphoreType.REGULAR((4,)), pltpu.SemaphoreType.REGULAR((4,)),
     ]
     hbm = pl.BlockSpec(memory_space=pl.ANY)
     return pl.pallas_call(

time: 60.2 us -> 56.2 us (0.934)
  Pallas kernels: 58.4 us -> 54.4 us
    pallas_call x1, Pallas kernels: 58.4 us -> 54.4 us  [body(): pl.pallas_call(functools.partial(kernel, gz, xy), out_shape=jax.ShapeDtyp...]
where the time goes in v2:
time: 56.2 us; the launch traced here: 56.1 us
  Pallas kernels  54.4 us (97%)
  local copies, waits for them, and re-layouts  1.67 us (3%)
    pallas_call x1, Pallas kernels, body(): pl.pallas_call(functools.partial(kernel, gz, xy), out_shape=jax.ShapeDtyp...  54.4 us
    unnamed x1, local copies, waits for them, and re-layouts  1.67 us

profile of v2, /device:TPU:1, one launch (start us, length us, event | category | flops | bytes accessed | tf_op | source)
XLA Modules:
  0.0 56.1 jit_solution(5696649922475931612)
XLA Ops:
  0.0 54.4 %vcycle.1 = f32[32,4,512]{2,1,0:T(4,128)} custom-call(f32[32,4,512]{2,1,0:T(4,128)} %src_hbm.1, f32[32,4,512]{2,1,0:T(4,128)} %pot_hbm.1, f32[256,512]{1,0:T(8,128)} %constant.8.clone.ty_hbm, f32[64,128]{1,0:T(8,128)} %constant.9.clone.fx_hbm, f32[256,128]{1,0:T(8,128)} %constant.10.clone.bx_hbm, f32[32,8,128]{2,1,0:T(8,128)} %constant.11.clone.th_hbm), custom_call_target="tpu_custom_call" | custom-call | tf_op jit(solution)/shard_map/vcycle/pallas_call | solution.py:404
  54.4 1.7 %copy.8 = f32[32,4,512]{2,1,0:T(4,128)} copy(f32[32,4,512]{2,1,0:T(4,128)} %vcycle.1) | data formatting | bytes 524288

commit v3 on v2

--- a/solution.py
+++ b/solution.py
@@ -3,6 +3,7 @@
 
 import jax
 import jax.numpy as jnp
+import ml_dtypes
 import numpy as np
 from jax import lax
 from jax.experimental import pallas as pl
@@ -13,7 +14,6 @@
 OMEGA = 0.8
 KAPPA = 1.0 / (SCREEN * SCREEN)
 CW = 6.0 + KAPPA
-HIGH = lax.Precision.HIGHEST
 M = 8
 CORNERS = ((-1, -1), (-1, 1), (1, -1), (1, 1))
 
@@ -26,6 +26,25 @@
 
 def eigen(count):
     return 2.0 - 2.0 * np.cos(math.pi / (count + 1) * np.arange(1, count + 1))
+
+
+def two_parts(table):
+    coarse = table.astype(ml_dtypes.bfloat16)
+    return np.stack([coarse, (table - coarse.astype(np.float64)).astype(ml_dtypes.bfloat16)])
+
+
+def dot3(value, table, dims):
+    coarse = value.astype(jnp.bfloat16)
+    fine = (value - coarse.astype(jnp.float32)).astype(jnp.bfloat16)
+    dot = lambda a, b: lax.dot_general(a, b, (dims, ((), ())), preferred_element_type=jnp.float32)
+    return dot(coarse, table[0]) + dot(fine, table[0]) + dot(coarse, table[1])
+
+
+def dot3_table_first(table, value, dims):
+    coarse = value.astype(jnp.bfloat16)
+    fine = (value - coarse.astype(jnp.float32)).astype(jnp.bfloat16)
+    dot = lambda a, b: lax.dot_general(a, b, (dims, ((), ())), preferred_element_type=jnp.float32)
+    return dot(table[0], coarse) + dot(table[0], fine) + dot(table[1], coarse)
 
 
 def tables(groups):
@@ -44,8 +63,7 @@
     diag = 2.0 + eigen(nx)[None, None, :] + eigen(ny).reshape(M, groups).T[:, :, None] + 4.0 * KAPPA
     theta = np.arccosh(0.5 * diag)
     theta = np.concatenate([theta, theta], axis=2)
-    f = lambda t: np.asarray(t, np.float32)
-    return f(ty), f(fx), f(bx.reshape(groups * 8, 2 * nx)), f(theta)
+    return two_parts(ty), two_parts(fx), two_parts(bx.reshape(groups * 8, 2 * nx)), theta.astype(np.float32)
 
 
 def kernel(
@@ -53,7 +71,7 @@
     potv, srcv, ty, fx, bx, th, pa, pb, sv,
     xps, xpr, xts, xtr, xss, xsr, zpr, zsr, cs, cr,
     xqs, xqr, zqr, ds, dr,
-    rs, s1, r1, fz, wz, ztile, zr, vz, s2, r2, cc,
+    rs, s1, r1, fz, wz, ztile, zr, vz, s2, r2, tm, cc,
     ld, e1s, e1r, e2s, e2r, a1s, a1r, gs, gr, a2s, a2r, known_x, known_z,
 ):
     q, me = lax.axis_index("gz"), lax.axis_index("xy")
@@ -69,9 +87,6 @@
         pltpu.make_async_copy(bx_hbm, bx, ld.at[4]),
         pltpu.make_async_copy(th_hbm.at[me], th, ld.at[5]),
     ]
-    for copy in loads:
-        copy.start()
-
     def shifted(dz, dx):
         where = {}
         if dz:
@@ -86,6 +101,8 @@
     barrier = pltpu.get_barrier_semaphore()
     for dz, dx in CORNERS + ((-1, 0), (1, 0), (0, -1), (0, 1)):
         tell(barrier, shifted(dz, dx))
+    loads[0].start()
+    loads[1].start()
 
     pa[...] = jnp.zeros_like(pa)
     sv[...] = jnp.zeros_like(sv)
@@ -162,6 +179,8 @@
     for c, (dz, dx) in enumerate(CORNERS):
         first.add(cs.at[c], cr.at[c], dz, dx)
     first.start()
+    for copy in loads[2:]:
+        copy.start()
 
     pa[3:top, 2:6, :] = potv[...]
     sv[2 : planes + 2, 2:6, :] = srcv[...]
@@ -218,7 +237,12 @@
             dst[i] = jnp.where(inside, relax(src, i, ends), 0.0)
             return carry
 
-        lax.fori_loop(3 - ring, top + ring, step, 0, unroll=2)
+        if ring == 2:
+            lax.fori_loop(1, top + 2, step, 0, unroll=4)
+        else:
+            lax.fori_loop(3, top, step, 0, unroll=4)
+            step(2, 0)
+            step(top, 0)
         for i in range(ring):
             dst[2 - i] = jnp.where(has_low, dst[2 - i], 0.0)
             dst[top + i] = jnp.where(has_high, dst[top + i], 0.0)
@@ -250,14 +274,11 @@
         return carry
 
     coarse = planes // 2
-    lax.fori_loop(0, coarse, coarsen, 0)
+    lax.fori_loop(0, coarse, coarsen, 0, unroll=2)
     for copy in loads[2:]:
         copy.wait()
     wide = coarse * 8
-    spec = lax.dot_general(
-        ty[...], rs[...].reshape(wide, ny), (((1,), (1,)), ((), ())),
-        precision=HIGH, preferred_element_type=jnp.float32,
-    )
+    spec = dot3_table_first(ty, rs[...].reshape(wide, ny), ((1,), (1,)))
     spec = spec + pltpu.roll(spec, wide - 1, 1)
     slot = lax.broadcasted_iota(jnp.int32, (xy, wide), 1) % 8
     for xx in range(2):
@@ -293,10 +314,7 @@
     round_of(4)
     everyone("xy", xy, me, lambda to: s1.at[to], r1, a1s, a1r)
     gathered = jnp.concatenate([r1[:, 0:1, :].reshape(xy, wide), r1[:, 1:2, :].reshape(xy, wide)], axis=0)
-    fz[...] = lax.dot_general(
-        gathered, fx[...], (((0,), (0,)), ((), ())),
-        precision=HIGH, preferred_element_type=jnp.float32,
-    ).reshape(coarse, M, 2 * half)
+    fz[...] = dot3(gathered.T, fx, ((1,), (0,))).reshape(coarse, M, 2 * half)
 
     up = lax.broadcasted_iota(jnp.int32, (M, 2 * half), 1) < half
     theta = th[...]
@@ -307,13 +325,13 @@
         wz[t] = state
     ztile[...] = state
     everyone("gz", gz, q, lambda to: ztile, zr, gs, gr)
-    block = jnp.exp(-float(coarse) * theta)
+    slab = jnp.exp(-float(coarse) * theta)
     total = jnp.zeros((M, 2 * half), jnp.float32)
     inflow = jnp.zeros((M, 2 * half), jnp.float32)
     steps_in = jnp.where(up, q, gz - 1 - q)
     for t in range(gz):
         inflow = jnp.where(steps_in == t, total, inflow)
-        total = block * total + jnp.where(up, zr[t], zr[gz - 1 - t])
+        total = slab * total + jnp.where(up, zr[t], zr[gz - 1 - t])
     span = float(coarse * gz + 1)
     image = pltpu.roll(total, half, 1) - jnp.exp(-span * theta) * total
     image = image * jnp.exp(-theta * (float(coarse) * steps_in.astype(jnp.float32) + 1.0))
@@ -330,29 +348,25 @@
     for z in range(coarse):
         value = scale * (wz[z] + pltpu.roll(wz[coarse - 1 - z], half, 1) - fz[z])
         ring = below if z == 0 else above if z == 1 else 0.0
-        vz[z] = jnp.where(up, value, ring)
-    s2[...] = lax.dot_general(
-        bx[...], vz[...].reshape(wide, 2 * half), (((1,), (1,)), ((), ())),
-        precision=HIGH, preferred_element_type=jnp.float32,
-    ).reshape(xy, 8, wide)
+        vz[pl.ds(z, M, stride=coarse), :] = jnp.where(up, value, ring)
+    s2[...] = dot3_table_first(bx, vz[...], ((1,), (1,))).reshape(xy, 8, wide)
     everyone("xy", xy, me, lambda to: s2.at[to], r2, a2s, a2r)
 
-    def spread(base):
-        parts = [r2[:, base + e : base + e + 1, :].reshape(xy, wide) for e in range(4)]
-        modes = []
-        for m in range(M):
-            mixed = jnp.zeros((xy, wide), jnp.float32)
-            for e in range(4):
-                shift = (2 * e - m) % wide
-                piece = pltpu.roll(parts[e], shift, 1) if shift else parts[e]
-                mixed = jnp.where(slot == 2 * e, piece, mixed)
-            modes.append(mixed + pltpu.roll(mixed, 1, 1))
-        return jnp.concatenate(modes, axis=0)
-
-    turned = jnp.concatenate([spread(0).T, spread(4).T[:16]], axis=0)
-    cc[...] = jnp.dot(
-        turned, ty[...], precision=HIGH, preferred_element_type=jnp.float32
-    ).reshape(coarse + 2, 8, ny)
+    block = lax.broadcasted_iota(jnp.int32, (coarse, half * 2), 1) // xy
+    for base, deep in ((0, coarse), (4, 8)):
+        turned = jnp.concatenate([r2[:, base + e : base + e + 1, :].reshape(xy, wide) for e in range(4)], axis=0).T
+        for e in range(4):
+            for j in range(2):
+                mixed = jnp.zeros((deep, 4 * xy), jnp.float32)
+                for b in range(4):
+                    at = (4 * j + b) * coarse
+                    piece, shift = turned[at : at + deep, :], (b - e) % 4 * xy
+                    piece = pltpu.roll(piece, shift, 1) if shift else piece
+                    mixed = jnp.where(block[:deep] == b, piece, mixed)
+                for twice in range(2):
+                    row, count = (2 * e + twice, coarse) if base == 0 else (wide + 2 * e + twice, 2)
+                    tm.at[j][pl.ds(row, count, stride=8), :] = mixed[:count]
+    cc[...] = dot3(jnp.concatenate([tm[0], tm[1]], axis=1), ty, ((1,), (0,))).reshape(coarse + 2, 8, ny)
 
     second.wait()
     pa[3:top, 0:2, :] = jnp.where(has_near, xqr[1], 0.0)
@@ -369,7 +383,7 @@
         pa[2 * z + 4] = pa[2 * z + 4] + fix
         return carry
 
-    lax.fori_loop(0, coarse, lift, 0)
+    lax.fori_loop(0, coarse, lift, 0, unroll=2)
     for i, z in ((1, coarse), (2, coarse), (top, coarse + 1), (top + 1, coarse + 1)):
         pa[i] = pa[i] + cc[z]
     sweep(pa, pb, 1)
@@ -378,7 +392,7 @@
         out_ref[i - 3] = relax(pb, i)[2:6, :]
         return carry
 
-    lax.fori_loop(3, top, last_sweep, 0, unroll=2)
+    lax.fori_loop(3, top, last_sweep, 0, unroll=4)
 
 
 def body(gz, xy, consts, source, potential):
@@ -387,16 +401,18 @@
     wide, two = coarse * 8, 4 * xy
     f32 = jnp.float32
     vm = lambda *shape: pltpu.VMEM(shape, f32)
+    half = lambda *shape: pltpu.VMEM((2, *shape), jnp.bfloat16)
     dma = lambda n: pltpu.SemaphoreType.DMA((n,))
     scratch = [
-        vm(planes, rows, ny), vm(planes, rows, ny), vm(M * xy, ny), vm(2 * xy, two), vm(8 * xy, two), vm(M, two),
+        vm(planes, rows, ny), vm(planes, rows, ny), half(M * xy, ny), half(2 * xy, two), half(8 * xy, two), vm(M, two),
         vm(planes + 6, 8, ny), vm(planes + 6, 8, ny), vm(planes + 4, 8, ny),
         vm(2, planes, 2, ny), vm(2, planes, 2, ny), vm(2, planes, 1, ny), vm(2, planes + 4, 1, ny),
         vm(2, planes, 2, ny), vm(2, planes, 2, ny),
         vm(2, 3, rows, ny), vm(2, 2, rows, ny), vm(4, 4, ny), vm(4, 4, ny),
         vm(2, planes, 2, ny), vm(2, planes, 2, ny), vm(2, 2, 8, ny), vm(4, 1, ny), vm(4, 1, ny),
         vm(coarse, 8, ny), vm(xy, 2, wide), vm(xy, 2, wide), vm(coarse, M, two), vm(coarse, M, two),
-        vm(M, two), vm(gz, M, two), vm(coarse, M, two), vm(xy, 8, wide), vm(xy, 8, wide), vm(coarse + 2, 8, ny),
+        vm(M, two), vm(gz, M, two), vm(wide, two), vm(xy, 8, wide), vm(xy, 8, wide),
+        vm(2, wide + 16, 4 * xy), vm(coarse + 2, 8, ny),
         dma(6), dma(14), dma(14), dma(8), dma(8), dma(xy), dma(xy), dma(gz), dma(gz), dma(xy), dma(xy),
         pltpu.SemaphoreType.REGULAR((4,)), pltpu.SemaphoreType.REGULAR((4,)),
     ]

time: 56.2 us -> 53.8 us (0.957)
  Pallas kernels: 54.4 us -> 51.9 us
    pallas_call x1, Pallas kernels: 54.4 us -> 51.9 us  [body(): pl.pallas_call(functools.partial(kernel, gz, xy), out_shape=jax.ShapeDtyp...]
where the time goes in v3:
time: 53.8 us; the launch traced here: 53.6 us
  Pallas kernels  51.9 us (96%)
  local copies, waits for them, and re-layouts  1.67 us (3%)
    pallas_call x1, Pallas kernels, body(): pl.pallas_call(functools.partial(kernel, gz, xy), out_shape=jax.ShapeDtyp...  51.9 us
    unnamed x1, local copies, waits for them, and re-layouts  1.67 us

profile of v3, /device:TPU:1, one launch (start us, length us, event | category | flops | bytes accessed | tf_op | source)
XLA Modules:
  0.0 53.6 jit_solution(3935741058318180994)
XLA Ops:
  0.0 51.9 %vcycle.1 = f32[32,4,512]{2,1,0:T(4,128)} custom-call(f32[32,4,512]{2,1,0:T(4,128)} %src_hbm.1, f32[32,4,512]{2,1,0:T(4,128)} %pot_hbm.1, bf16[2,256,512]{2,1,0:T(8,128)(2,1)} %constant.8.clone.ty_hbm, bf16[2,64,128]{2,1,0:T(8,128)(2,1)} %constant.9.clone.fx_hbm, bf16[2,256,128]{2,1,0:T(8,128)(2,1)} %constant.10.clone.bx_hbm, ...), custom_call_target="tpu_custom_call" | custom-call | tf_op jit(solution)/shard_map/vcycle/pallas_call | solution.py:420
  51.9 1.7 %copy.8 = f32[32,4,512]{2,1,0:T(4,128)} copy(f32[32,4,512]{2,1,0:T(4,128)} %vcycle.1) | data formatting | bytes 524288

commit v4 on v3

--- a/solution.py
+++ b/solution.py
@@ -67,12 +67,12 @@
 
 
 def kernel(
-    gz, xy, src_hbm, pot_hbm, ty_hbm, fx_hbm, bx_hbm, th_hbm, out_ref,
+    gz, xy, src_hbm, pot_hbm, ty_hbm, fx_hbm, bx_hbm, th_hbm, out_hbm,
     potv, srcv, ty, fx, bx, th, pa, pb, sv,
     xps, xpr, xts, xtr, xss, xsr, zpr, zsr, cs, cr,
     xqs, xqr, zqr, ds, dr,
     rs, s1, r1, fz, wz, ztile, zr, vz, s2, r2, tm, cc,
-    ld, e1s, e1r, e2s, e2r, a1s, a1r, gs, gr, a2s, a2r, known_x, known_z,
+    ld, e1s, e1r, e2s, e2r, a1s, a1r, gs, gr, a2s, a2r, outs, known_x, known_z,
 ):
     q, me = lax.axis_index("gz"), lax.axis_index("xy")
     planes, rows, ny = potv.shape
@@ -146,9 +146,9 @@
             copy = remote(src, dst, self.send.at[slot], self.recv.at[slot], shifted(dz, dx))
             self.copies.append((copy, exists(dz, dx), exists(-dz, -dx)))
 
-        def start(self):
-            for copy, there, unused in self.copies:
-                pl.when(there)(copy.start)
+        def start(self, slot):
+            copy, there, unused = self.copies[slot]
+            pl.when(there)(copy.start)
 
         def wait(self):
             for copy, there, back in self.copies:
@@ -178,7 +178,8 @@
         first.add(srcv.at[pl.ds(0 if step < 0 else planes - 2, 2)], zsr.at[side], step, 0)
     for c, (dz, dx) in enumerate(CORNERS):
         first.add(cs.at[c], cr.at[c], dz, dx)
-    first.start()
+    for slot in range(len(first.copies)):
+        first.start(slot)
     for copy in loads[2:]:
         copy.start()
 
@@ -196,8 +197,10 @@
         x0, x1 = (6, 7) if dx < 0 else (1, 0)
         return z0, z1, x0, x1, exists(-dz, -dx)
 
+    round_of(1)
+    round_of(2)
     first.wait()
-    round_of(1)
+    round_of(3)
     pa[3:top, 0:2, :] = jnp.where(has_near, xpr[1], 0.0)
     pa[3:top, 6:8, :] = jnp.where(has_far, xpr[0], 0.0)
     pa[0:3, 2:6, :] = jnp.where(has_low, zpr[1], 0.0)
@@ -248,8 +251,8 @@
             dst[top + i] = jnp.where(has_high, dst[top + i], 0.0)
 
     sweep(pa, pb, 2, True)
-    round_of(2)
     sweep(pb, pa, 1)
+    round_of(4)
 
     xqs[0] = pa[3:top, 2:4, :]
     xqs[1] = pa[3:top, 4:6, :]
@@ -262,8 +265,8 @@
         second.add(pa.at[pl.ds(3 if step < 0 else top - 2, 2)], zqr.at[side], step, 0)
     for c, (dz, dx) in enumerate(CORNERS):
         second.add(ds.at[c], dr.at[c], dz, dx)
-    second.start()
-    round_of(3)
+    for slot in (1, 3, 4, 5, 6, 7):
+        second.start(slot)
 
     def residual(i):
         v, total = neighbours(pa, i)
@@ -290,29 +293,25 @@
             packed = jnp.where(slot == m, piece, packed)
         s1[:, xx : xx + 1, :] = packed.reshape(xy, 1, wide)
 
-    def everyone(axis, size, mine, src_of, dst, send, recv):
-        def copy_to(i):
+    def everyone(axis, size, mine, far, src_of, dst, send, recv):
+        for i in sorted(range(1, size), key=far, reverse=True):
             to = lax.rem(mine + i, size)
-            return remote(src_of(to), dst.at[mine], send.at[to], recv.at[mine], {axis: to})
-
-        def copy_from(i):
-            to = lax.rem(mine + i, size)
-            return remote(src_of(to), dst.at[to], send.at[to], recv.at[to], {axis: to})
-
-        def go(i, carry):
-            copy_to(i).start()
-            return carry
-
-        def done(i, carry):
-            copy_from(i).wait()
-            return carry
-
-        lax.fori_loop(1, size, go, 0)
+            remote(src_of(to), dst.at[mine], send.at[0], recv.at[0], {axis: to}).start()
         dst[mine] = src_of(mine)[...]
-        lax.fori_loop(1, size, done, 0)
-
-    round_of(4)
-    everyone("xy", xy, me, lambda to: s1.at[to], r1, a1s, a1r)
+        rest = dst.at[pl.ds(0, size - 1)]
+        done = remote(rest, rest, send.at[0], recv.at[0], {axis: lax.rem(mine + 1, size)})
+        done.wait_recv()
+        done.wait_send()
+
+    def hops_xy(i):
+        return min(i // 8, 4 - i // 8) + min(i % 8 // 2, 4 - i % 8 // 2)
+
+    def hops_z(i):
+        return min(i, gz - i)
+
+    everyone("xy", xy, me, hops_xy, lambda to: s1.at[to], r1, a1s, a1r)
+    second.start(0)
+    second.start(2)
     gathered = jnp.concatenate([r1[:, 0:1, :].reshape(xy, wide), r1[:, 1:2, :].reshape(xy, wide)], axis=0)
     fz[...] = dot3(gathered.T, fx, ((1,), (0,))).reshape(coarse, M, 2 * half)
 
@@ -324,7 +323,7 @@
         state = decay * state + jnp.where(up, fz[t], fz[coarse - 1 - t])
         wz[t] = state
     ztile[...] = state
-    everyone("gz", gz, q, lambda to: ztile, zr, gs, gr)
+    everyone("gz", gz, q, hops_z, lambda to: ztile, zr, gs, gr)
     slab = jnp.exp(-float(coarse) * theta)
     total = jnp.zeros((M, 2 * half), jnp.float32)
     inflow = jnp.zeros((M, 2 * half), jnp.float32)
@@ -350,7 +349,7 @@
         ring = below if z == 0 else above if z == 1 else 0.0
         vz[pl.ds(z, M, stride=coarse), :] = jnp.where(up, value, ring)
     s2[...] = dot3_table_first(bx, vz[...], ((1,), (1,))).reshape(xy, 8, wide)
-    everyone("xy", xy, me, lambda to: s2.at[to], r2, a2s, a2r)
+    everyone("xy", xy, me, hops_xy, lambda to: s2.at[to], r2, a2s, a2r)
 
     block = lax.broadcasted_iota(jnp.int32, (coarse, half * 2), 1) // xy
     for base, deep in ((0, coarse), (4, 8)):
@@ -389,10 +388,18 @@
     sweep(pa, pb, 1)
 
     def last_sweep(i, carry):
-        out_ref[i - 3] = relax(pb, i)[2:6, :]
+        potv[i - 3] = relax(pb, i)[2:6, :]
         return carry
 
-    lax.fori_loop(3, top, last_sweep, 0, unroll=4)
+    part = planes // 4
+    leaving = []
+    for c in range(4):
+        lax.fori_loop(3 + c * part, 3 + (c + 1) * part, last_sweep, 0, unroll=4)
+        here = pl.ds(c * part, part)
+        leaving.append(pltpu.make_async_copy(potv.at[here], out_hbm.at[here], outs.at[c]))
+        leaving[-1].start()
+    for copy in leaving:
+        copy.wait()
 
 
 def body(gz, xy, consts, source, potential):
@@ -413,19 +420,19 @@
         vm(coarse, 8, ny), vm(xy, 2, wide), vm(xy, 2, wide), vm(coarse, M, two), vm(coarse, M, two),
         vm(M, two), vm(gz, M, two), vm(wide, two), vm(xy, 8, wide), vm(xy, 8, wide),
         vm(2, wide + 16, 4 * xy), vm(coarse + 2, 8, ny),
-        dma(6), dma(14), dma(14), dma(8), dma(8), dma(xy), dma(xy), dma(gz), dma(gz), dma(xy), dma(xy),
+        dma(6), dma(14), dma(14), dma(8), dma(8), dma(1), dma(1), dma(1), dma(1), dma(1), dma(1), dma(4),
         pltpu.SemaphoreType.REGULAR((4,)), pltpu.SemaphoreType.REGULAR((4,)),
     ]
     hbm = pl.BlockSpec(memory_space=pl.ANY)
     return pl.pallas_call(
         functools.partial(kernel, gz, xy),
         out_shape=jax.ShapeDtypeStruct(source.shape, f32),
-        in_specs=[hbm] * 6,
-        out_specs=pl.BlockSpec(memory_space=pltpu.VMEM),
+        in_specs=[pl.BlockSpec(memory_space=pltpu.HBM)] * 6,
+        out_specs=hbm,
         scratch_shapes=scratch,
-        compiler_params=pltpu.CompilerParams(collective_id=0, has_side_effects=True),
+        compiler_params=pltpu.CompilerParams(vmem_limit_bytes=24 * 1024 * 1024, collective_id=0, has_side_effects=True),
         name="vcycle",
-    )(source, potential, *[jnp.asarray(c) for c in consts])
+    )(*[pltpu.with_memory_space_constraint(a, pltpu.HBM) for a in (source, potential, *map(jnp.asarray, consts))])
 
 
 def solution(mesh):

time: 53.8 us -> 48.6 us (0.903)
  Pallas kernels: 51.9 us -> 47.8 us
  local copies, waits for them, and re-layouts: 1.67 us -> 0.71 us
    pallas_call x1, Pallas kernels: 51.9 us -> 47.8 us  [body(): pl.pallas_call(functools.partial(kernel, gz, xy), out_shape=jax.ShapeDtyp...]
    unnamed x1, local copies, waits for them, and re-layouts: 1.67 us -> 0.71 us
where the time goes in v4:
time: 48.6 us; the launch traced here: 48.5 us
  Pallas kernels  47.8 us (98%)
  local copies, waits for them, and re-layouts  0.71 us (1%)
    pallas_call x1, Pallas kernels, body(): pl.pallas_call(functools.partial(kernel, gz, xy), out_shape=jax.ShapeDtyp...  47.8 us

profile of v4, /device:TPU:1, one launch (start us, length us, event | category | flops | bytes accessed | tf_op | source)
XLA Modules:
  0.0 48.5 jit_solution(163511073575456414)
XLA Ops:
  0.0 47.8 %vcycle.1 = f32[32,4,512]{2,1,0:T(4,128)S(1)} custom-call(f32[32,4,512]{2,1,0:T(4,128)} %src_hbm.1, f32[32,4,512]{2,1,0:T(4,128)} %pot_hbm.1, bf16[2,256,512]{2,1,0:T(8,128)(2,1)} %constant.8.clone.ty_hbm, bf16[2,64,128]{2,1,0:T(8,128)(2,1)} %constant.9.clone.fx_hbm, bf16[2,256,128]{2,1,0:T(8,128)(2,1)} %constant.10.clone.bx_hbm, ...), custom_call_target="tpu_custom_call" | custom-call | tf_op jit(solution)/shard_map/vcycle/pallas_call | solution.py:427
  47.8 0.7 %copy.8 = f32[32,4,512]{2,1,0:T(4,128)} copy(f32[32,4,512]{2,1,0:T(4,128)S(1)} %vcycle.1) | data formatting | bytes 524288

commit v5 on v4

--- a/solution.py
+++ b/solution.py
@@ -104,17 +104,70 @@
     loads[0].start()
     loads[1].start()
 
-    pa[...] = jnp.zeros_like(pa)
-    sv[...] = jnp.zeros_like(sv)
     for side in range(2):
         xtr[side, 0:2] = jnp.zeros((2, 1, ny), jnp.float32)
         xtr[side, planes + 2 : planes + 4] = jnp.zeros((2, 1, ny), jnp.float32)
     loads[0].wait()
-    loads[1].wait()
     xps[0] = potv[:, 0:2, :]
     xps[1] = potv[:, 2:4, :]
     xts[0] = potv[:, 2:3, :]
     xts[1] = potv[:, 1:2, :]
+    pl.semaphore_wait(barrier, 8)
+
+    def round_of(level):
+        for axis, size, dim, known in (("xy", xy, 1, known_x), ("gz", gz, 0, known_z)):
+            reach = 2**level
+            if level and reach // 2 < size // 2:
+                pl.semaphore_wait(known.at[level - 1], 2)
+            if reach < size // 2:
+                for way in (-reach, reach):
+                    tell(known.at[level], shifted(way, 0) if dim == 0 else shifted(0, way))
+
+    class Exchange:
+        def __init__(self, send, recv):
+            self.send, self.recv, self.copies = send, recv, []
+
+        def add(self, src, dst, dz, dx):
+            slot = len(self.copies)
+            copy = remote(src, dst, self.send.at[slot], self.recv.at[slot], shifted(dz, dx))
+            self.copies.append((copy, exists(dz, dx), exists(-dz, -dx)))
+
+        def start(self, slot):
+            copy, there, unused = self.copies[slot]
+            pl.when(there)(copy.start)
+
+        def wait(self):
+            for copy, there, back in self.copies:
+                pl.when(back)(copy.wait_recv)
+                pl.when(there)(copy.wait_send)
+
+    def exists(dz, dx):
+        there = None
+        for step, mine, size in ((dz, q, gz), (dx, me, xy)):
+            if step:
+                ok = mine > 0 if step < 0 else mine < size - 1
+                there = ok if there is None else jnp.logical_and(there, ok)
+        return there
+
+    def remote(src, dst, send, recv, where):
+        return pltpu.make_async_remote_copy(
+            src_ref=src, dst_ref=dst, send_sem=send, recv_sem=recv,
+            device_id=where, device_id_type=pl.DeviceIdType.MESH,
+        )
+
+    first = Exchange(e1s, e1r)
+    for side, step in ((0, -1), (1, 1)):
+        first.add(xps.at[side], xpr.at[side], 0, step)
+        first.add(xts.at[side], xtr.at[side, pl.ds(2, planes)], 0, step)
+        first.add(xss.at[side], xsr.at[side], 0, step)
+        first.add(potv.at[pl.ds(0 if step < 0 else planes - 3, 3)], zpr.at[side], step, 0)
+        first.add(srcv.at[pl.ds(0 if step < 0 else planes - 2, 2)], zsr.at[side], step, 0)
+    for c, (dz, dx) in enumerate(CORNERS):
+        first.add(cs.at[c], cr.at[c], dz, dx)
+    for slot in (0, 5, 1, 6, 3, 8):
+        first.start(slot)
+    round_of(0)
+    loads[1].wait()
     xss[0] = srcv[:, 0:2, :]
     xss[1] = srcv[:, 2:4, :]
     for c, (dz, dx) in enumerate(CORNERS):
@@ -124,65 +177,13 @@
         cs[c, 1:2] = potv[z0, x1 : x1 + 1, :]
         cs[c, 2:3] = potv[z1, x0 : x0 + 1, :]
         cs[c, 3:4] = srcv[z0, x0 : x0 + 1, :]
-    pl.semaphore_wait(barrier, 8)
-
-    def round_of(level):
-        for axis, size, dim, known in (("xy", xy, 1, known_x), ("gz", gz, 0, known_z)):
-            reach = 2**level
-            if level and reach // 2 < size // 2:
-                pl.semaphore_wait(known.at[level - 1], 2)
-            if reach < size // 2:
-                for way in (-reach, reach):
-                    tell(known.at[level], shifted(way, 0) if dim == 0 else shifted(0, way))
-
-    round_of(0)
-
-    class Exchange:
-        def __init__(self, send, recv):
-            self.send, self.recv, self.copies = send, recv, []
-
-        def add(self, src, dst, dz, dx):
-            slot = len(self.copies)
-            copy = remote(src, dst, self.send.at[slot], self.recv.at[slot], shifted(dz, dx))
-            self.copies.append((copy, exists(dz, dx), exists(-dz, -dx)))
-
-        def start(self, slot):
-            copy, there, unused = self.copies[slot]
-            pl.when(there)(copy.start)
-
-        def wait(self):
-            for copy, there, back in self.copies:
-                pl.when(back)(copy.wait_recv)
-                pl.when(there)(copy.wait_send)
-
-    def exists(dz, dx):
-        there = None
-        for step, mine, size in ((dz, q, gz), (dx, me, xy)):
-            if step:
-                ok = mine > 0 if step < 0 else mine < size - 1
-                there = ok if there is None else jnp.logical_and(there, ok)
-        return there
-
-    def remote(src, dst, send, recv, where):
-        return pltpu.make_async_remote_copy(
-            src_ref=src, dst_ref=dst, send_sem=send, recv_sem=recv,
-            device_id=where, device_id_type=pl.DeviceIdType.MESH,
-        )
-
-    first = Exchange(e1s, e1r)
-    for side, step in ((0, -1), (1, 1)):
-        first.add(xps.at[side], xpr.at[side], 0, step)
-        first.add(xts.at[side], xtr.at[side, pl.ds(2, planes)], 0, step)
-        first.add(xss.at[side], xsr.at[side], 0, step)
-        first.add(potv.at[pl.ds(0 if step < 0 else planes - 3, 3)], zpr.at[side], step, 0)
-        first.add(srcv.at[pl.ds(0 if step < 0 else planes - 2, 2)], zsr.at[side], step, 0)
-    for c, (dz, dx) in enumerate(CORNERS):
-        first.add(cs.at[c], cr.at[c], dz, dx)
-    for slot in range(len(first.copies)):
+    for slot in (2, 7, 4, 9, 10, 11, 12, 13):
         first.start(slot)
     for copy in loads[2:]:
         copy.start()
 
+    pa[...] = jnp.zeros_like(pa)
+    sv[...] = jnp.zeros_like(sv)
     pa[3:top, 2:6, :] = potv[...]
     sv[2 : planes + 2, 2:6, :] = srcv[...]
     sub = lax.broadcasted_iota(jnp.int32, (8, ny), 0)
@@ -293,11 +294,13 @@
             packed = jnp.where(slot == m, piece, packed)
         s1[:, xx : xx + 1, :] = packed.reshape(xy, 1, wide)
 
-    def everyone(axis, size, mine, far, src_of, dst, send, recv):
+    def everyone(axis, size, mine, far, src_of, dst, send, recv, meanwhile=None):
         for i in sorted(range(1, size), key=far, reverse=True):
             to = lax.rem(mine + i, size)
             remote(src_of(to), dst.at[mine], send.at[0], recv.at[0], {axis: to}).start()
         dst[mine] = src_of(mine)[...]
+        if meanwhile is not None:
+            meanwhile()
         rest = dst.at[pl.ds(0, size - 1)]
         done = remote(rest, rest, send.at[0], recv.at[0], {axis: lax.rem(mine + 1, size)})
         done.wait_recv()
@@ -349,7 +352,17 @@
         ring = below if z == 0 else above if z == 1 else 0.0
         vz[pl.ds(z, M, stride=coarse), :] = jnp.where(up, value, ring)
     s2[...] = dot3_table_first(bx, vz[...], ((1,), (1,))).reshape(xy, 8, wide)
-    everyone("xy", xy, me, hops_xy, lambda to: s2.at[to], r2, a2s, a2r)
+    def second_halo():
+        second.wait()
+        pa[3:top, 0:2, :] = jnp.where(has_near, xqr[1], 0.0)
+        pa[3:top, 6:8, :] = jnp.where(has_far, xqr[0], 0.0)
+        pa[1:3, 2:6, :] = jnp.where(has_low, zqr[1, :, 2:6, :], 0.0)
+        pa[top : top + 2, 2:6, :] = jnp.where(has_high, zqr[0, :, 2:6, :], 0.0)
+        for c, (dz, dx) in enumerate(CORNERS):
+            z0, z1, x0, x1, there = corner_places(dz, dx)
+            pa[z0, x0 : x0 + 1, :] = jnp.where(there, dr[c], 0.0)
+
+    everyone("xy", xy, me, hops_xy, lambda to: s2.at[to], r2, a2s, a2r, second_halo)
 
     block = lax.broadcasted_iota(jnp.int32, (coarse, half * 2), 1) // xy
     for base, deep in ((0, coarse), (4, 8)):
@@ -366,15 +379,6 @@
                     row, count = (2 * e + twice, coarse) if base == 0 else (wide + 2 * e + twice, 2)
                     tm.at[j][pl.ds(row, count, stride=8), :] = mixed[:count]
     cc[...] = dot3(jnp.concatenate([tm[0], tm[1]], axis=1), ty, ((1,), (0,))).reshape(coarse + 2, 8, ny)
-
-    second.wait()
-    pa[3:top, 0:2, :] = jnp.where(has_near, xqr[1], 0.0)
-    pa[3:top, 6:8, :] = jnp.where(has_far, xqr[0], 0.0)
-    pa[1:3, 2:6, :] = jnp.where(has_low, zqr[1, :, 2:6, :], 0.0)
-    pa[top : top + 2, 2:6, :] = jnp.where(has_high, zqr[0, :, 2:6, :], 0.0)
-    for c, (dz, dx) in enumerate(CORNERS):
-        z0, z1, x0, x1, there = corner_places(dz, dx)
-        pa[z0, x0 : x0 + 1, :] = jnp.where(there, dr[c], 0.0)
 
     def lift(z, carry):
         fix = cc[z]

time: 48.6 us -> 48.5 us (level)
  no operation moved by 1% of the time
where the time goes in v5:
time: 48.5 us; the launch traced here: 48.4 us
  Pallas kernels  47.7 us (98%)
  local copies, waits for them, and re-layouts  0.71 us (1%)
    pallas_call x1, Pallas kernels, body(): pl.pallas_call(functools.partial(kernel, gz, xy), out_shape=jax.ShapeDtyp...  47.7 us

profile of v5, /device:TPU:1, one launch (start us, length us, event | category | flops | bytes accessed | tf_op | source)
XLA Modules:
  0.0 48.4 jit_solution(877882582661782521)
XLA Ops:
  0.0 47.7 %vcycle.1 = f32[32,4,512]{2,1,0:T(4,128)S(1)} custom-call(f32[32,4,512]{2,1,0:T(4,128)} %src_hbm.1, f32[32,4,512]{2,1,0:T(4,128)} %pot_hbm.1, bf16[2,256,512]{2,1,0:T(8,128)(2,1)} %constant.8.clone.ty_hbm, bf16[2,64,128]{2,1,0:T(8,128)(2,1)} %constant.9.clone.fx_hbm, bf16[2,256,128]{2,1,0:T(8,128)(2,1)} %constant.10.clone.bx_hbm, ...), custom_call_target="tpu_custom_call" | custom-call | tf_op jit(solution)/shard_map/vcycle/pallas_call | solution.py:431
  47.7 0.7 %copy.8 = f32[32,4,512]{2,1,0:T(4,128)} copy(f32[32,4,512]{2,1,0:T(4,128)S(1)} %vcycle.1) | data formatting | bytes 524288

commit v6 on v5

--- a/solution.py
+++ b/solution.py
@@ -218,16 +218,20 @@
         pa[z1, x0 : x0 + 1, :] = corner[2:3]
         sv[z0 - 1, x0 : x0 + 1, :] = corner[3:4]
 
+    def row_sum(v):
+        before = jnp.where(lane == 0, 0.0, pltpu.roll(v, 1, 1))
+        return before + jnp.where(lane == ny - 1, 0.0, pltpu.roll(v, ny - 1, 1))
+
+    def flat_sum(v):
+        return pltpu.roll(v, 1, 0) + pltpu.roll(v, 7, 0) + row_sum(v)
+
     def neighbours(ref, i, ends=None):
         v = ref[i]
         total = ref[i - 1] + ref[i + 1]
         back, forth = pltpu.roll(v, 1, 0), pltpu.roll(v, 7, 0)
         if ends is not None:
             back, forth = jnp.where(sub == 0, ends[0], back), jnp.where(sub == 7, ends[1], forth)
-        total = total + back + forth
-        total = total + jnp.where(lane == 0, 0.0, pltpu.roll(v, 1, 1))
-        total = total + jnp.where(lane == ny - 1, 0.0, pltpu.roll(v, ny - 1, 1))
-        return v, total
+        return v, total + back + forth + row_sum(v)
 
     def relax(ref, i, ends=None):
         v, total = neighbours(ref, i, ends)
@@ -362,6 +366,14 @@
             z0, z1, x0, x1, there = corner_places(dz, dx)
             pa[z0, x0 : x0 + 1, :] = jnp.where(there, dr[c], 0.0)
 
+        sweep(pa, pb, 1)
+
+        def base_sweep(i, carry):
+            pa[i] = relax(pb, i)
+            return carry
+
+        lax.fori_loop(3, top, base_sweep, 0, unroll=4)
+
     everyone("xy", xy, me, hops_xy, lambda to: s2.at[to], r2, a2s, a2r, second_halo)
 
     block = lax.broadcasted_iota(jnp.int32, (coarse, half * 2), 1) // xy
@@ -378,21 +390,31 @@
                 for twice in range(2):
                     row, count = (2 * e + twice, coarse) if base == 0 else (wide + 2 * e + twice, 2)
                     tm.at[j][pl.ds(row, count, stride=8), :] = mixed[:count]
-    cc[...] = dot3(jnp.concatenate([tm[0], tm[1]], axis=1), ty, ((1,), (0,))).reshape(coarse + 2, 8, ny)
-
-    def lift(z, carry):
-        fix = cc[z]
-        pa[2 * z + 3] = pa[2 * z + 3] + fix
-        pa[2 * z + 4] = pa[2 * z + 4] + fix
+    fixes = dot3(jnp.concatenate([tm[0], tm[1]], axis=1), ty, ((1,), (0,))).reshape(coarse + 2, 8, ny)
+    cc[1 : coarse + 1] = fixes[:coarse]
+    cc[0] = fixes[coarse]
+    cc[coarse + 1] = fixes[coarse + 1]
+
+    gain = OMEGA / CW
+
+    def shared(z):
+        v = cc[z]
+        total = v + flat_sum(v)
+        return (1.0 - OMEGA) * v + gain * total
+
+    def lifted_sweep(z, carry):
+        common = shared(z)
+        pb[2 * z + 1] = jnp.where(inside, common + gain * cc[z - 1], 0.0)
+        pb[2 * z + 2] = jnp.where(inside, common + gain * cc[z + 1], 0.0)
         return carry
 
-    lax.fori_loop(0, coarse, lift, 0, unroll=2)
-    for i, z in ((1, coarse), (2, coarse), (top, coarse + 1), (top + 1, coarse + 1)):
-        pa[i] = pa[i] + cc[z]
-    sweep(pa, pb, 1)
+    lax.fori_loop(1, coarse + 1, lifted_sweep, 0, unroll=2)
+    pb[2] = jnp.where(jnp.logical_and(inside, has_low), shared(0) + gain * cc[1], 0.0)
+    pb[top] = jnp.where(jnp.logical_and(inside, has_high), shared(coarse + 1) + gain * cc[coarse], 0.0)
 
     def last_sweep(i, carry):
-        potv[i - 3] = relax(pb, i)[2:6, :]
+        v, total = neighbours(pb, i)
+        potv[i - 3] = (pa[i] + (1.0 - OMEGA) * v + gain * total)[2:6, :]
         return carry
 
     part = planes // 4

time: 48.5 us -> 48.3 us (level)
  no operation moved by 1% of the time
where the time goes in v6:
time: 48.3 us; the launch traced here: 48.2 us
  Pallas kernels  47.5 us (98%)
  local copies, waits for them, and re-layouts  0.71 us (1%)
    pallas_call x1, Pallas kernels, body(): pl.pallas_call(functools.partial(kernel, gz, xy), out_shape=jax.ShapeDtyp...  47.5 us

profile of v6, /device:TPU:1, one launch (start us, length us, event | category | flops | bytes accessed | tf_op | source)
XLA Modules:
  0.0 48.2 jit_solution(15058618931671491103)
XLA Ops:
  0.0 47.5 %vcycle.1 = f32[32,4,512]{2,1,0:T(4,128)S(1)} custom-call(f32[32,4,512]{2,1,0:T(4,128)} %src_hbm.1, f32[32,4,512]{2,1,0:T(4,128)} %pot_hbm.1, bf16[2,256,512]{2,1,0:T(8,128)(2,1)} %constant.8.clone.ty_hbm, bf16[2,64,128]{2,1,0:T(8,128)(2,1)} %constant.9.clone.fx_hbm, bf16[2,256,128]{2,1,0:T(8,128)(2,1)} %constant.10.clone.bx_hbm, ...), custom_call_target="tpu_custom_call" | custom-call | tf_op jit(solution)/shard_map/vcycle/pallas_call | solution.py:453
  47.5 0.7 %copy.8 = f32[32,4,512]{2,1,0:T(4,128)} copy(f32[32,4,512]{2,1,0:T(4,128)S(1)} %vcycle.1) | data formatting | bytes 524288

commit v7 on v6

--- a/solution.py
+++ b/solution.py
@@ -201,7 +201,6 @@
     round_of(1)
     round_of(2)
     first.wait()
-    round_of(3)
     pa[3:top, 0:2, :] = jnp.where(has_near, xpr[1], 0.0)
     pa[3:top, 6:8, :] = jnp.where(has_far, xpr[0], 0.0)
     pa[0:3, 2:6, :] = jnp.where(has_low, zpr[1], 0.0)
@@ -256,8 +255,8 @@
             dst[top + i] = jnp.where(has_high, dst[top + i], 0.0)
 
     sweep(pa, pb, 2, True)
+    round_of(3)
     sweep(pb, pa, 1)
-    round_of(4)
 
     xqs[0] = pa[3:top, 2:4, :]
     xqs[1] = pa[3:top, 4:6, :]
@@ -316,6 +315,7 @@
     def hops_z(i):
         return min(i, gz - i)
 
+    round_of(4)
     everyone("xy", xy, me, hops_xy, lambda to: s1.at[to], r1, a1s, a1r)
     second.start(0)
     second.start(2)

time: 48.3 us -> 47.1 us (0.975)
  Pallas kernels: 47.5 us -> 46.3 us
    pallas_call x1, Pallas kernels: 47.5 us -> 46.3 us  [body(): pl.pallas_call(functools.partial(kernel, gz, xy), out_shape=jax.ShapeDtyp...]
where the time goes in v7:
time: 47.1 us; the launch traced here: 47 us
  Pallas kernels  46.3 us (98%)
  local copies, waits for them, and re-layouts  0.71 us (2%)
    pallas_call x1, Pallas kernels, body(): pl.pallas_call(functools.partial(kernel, gz, xy), out_shape=jax.ShapeDtyp...  46.3 us

profile of v7, /device:TPU:1, one launch (start us, length us, event | category | flops | bytes accessed | tf_op | source)
XLA Modules:
  0.0 47.0 jit_solution(2924025476674623833)
XLA Ops:
  0.0 46.3 %vcycle.1 = f32[32,4,512]{2,1,0:T(4,128)S(1)} custom-call(f32[32,4,512]{2,1,0:T(4,128)} %src_hbm.1, f32[32,4,512]{2,1,0:T(4,128)} %pot_hbm.1, bf16[2,256,512]{2,1,0:T(8,128)(2,1)} %constant.8.clone.ty_hbm, bf16[2,64,128]{2,1,0:T(8,128)(2,1)} %constant.9.clone.fx_hbm, bf16[2,256,128]{2,1,0:T(8,128)(2,1)} %constant.10.clone.bx_hbm, ...), custom_call_target="tpu_custom_call" | custom-call | tf_op jit(solution)/shard_map/vcycle/pallas_call | solution.py:453
  46.3 0.7 %copy.8 = f32[32,4,512]{2,1,0:T(4,128)} copy(f32[32,4,512]{2,1,0:T(4,128)S(1)} %vcycle.1) | data formatting | bytes 524288

commit v8 on v7

--- a/solution.py
+++ b/solution.py
@@ -255,8 +255,9 @@
             dst[top + i] = jnp.where(has_high, dst[top + i], 0.0)
 
     sweep(pa, pb, 2, True)
+
+    sweep(pb, pa, 1)
     round_of(3)
-    sweep(pb, pa, 1)
 
     xqs[0] = pa[3:top, 2:4, :]
     xqs[1] = pa[3:top, 4:6, :]

time: 47.1 us -> 46.2 us (0.981)
  Pallas kernels: 46.3 us -> 45.4 us
    pallas_call x1, Pallas kernels: 46.3 us -> 45.4 us  [body(): pl.pallas_call(functools.partial(kernel, gz, xy), out_shape=jax.ShapeDtyp...]
where the time goes in v8:
time: 46.2 us; the launch traced here: 46.1 us
  Pallas kernels  45.4 us (98%)
  local copies, waits for them, and re-layouts  0.71 us (2%)
    pallas_call x1, Pallas kernels, body(): pl.pallas_call(functools.partial(kernel, gz, xy), out_shape=jax.ShapeDtyp...  45.4 us

profile of v8, /device:TPU:1, one launch (start us, length us, event | category | flops | bytes accessed | tf_op | source)
XLA Modules:
  0.0 46.1 jit_solution(917883351765827582)
XLA Ops:
  0.0 45.4 %vcycle.1 = f32[32,4,512]{2,1,0:T(4,128)S(1)} custom-call(f32[32,4,512]{2,1,0:T(4,128)} %src_hbm.1, f32[32,4,512]{2,1,0:T(4,128)} %pot_hbm.1, bf16[2,256,512]{2,1,0:T(8,128)(2,1)} %constant.8.clone.ty_hbm, bf16[2,64,128]{2,1,0:T(8,128)(2,1)} %constant.9.clone.fx_hbm, bf16[2,256,128]{2,1,0:T(8,128)(2,1)} %constant.10.clone.bx_hbm, ...), custom_call_target="tpu_custom_call" | custom-call | tf_op jit(solution)/shard_map/vcycle/pallas_call | solution.py:454
  45.4 0.7 %copy.8 = f32[32,4,512]{2,1,0:T(4,128)} copy(f32[32,4,512]{2,1,0:T(4,128)S(1)} %vcycle.1) | data formatting | bytes 524288
